TPU v7x, 512 devices: a whole 4x8x8 slice. The times are simulated.
512 devices in a mesh: grp: 32 (over x_hi, y, core), die: 16 (over x_lo, z).
Axes of the slice: x: 4 (x_hi: 2, x_lo: 2; x = x_hi * 2 + x_lo), y: 8, z: 8, core: 2. Of those that a mesh axis runs over, the one named last changes fastest.
Arguments:
- die_volt: float32 [4096, 4096], P('grp', 'die'), may hold values from -6 to 6
- die_load: float32 [4096, 4096], P('grp', 'die'), may hold values from 0.05 to 1
- die_shunt: float32 [4096, 4096], P('grp', 'die'), may hold values from 0.1 to 1
- bump_node: int32 [32768, 128], P(('grp', 'die')), may hold values from -1 to 32767, as said below
- bump_block: int32 [32768], P(('grp', 'die')), may hold values from 0 to 16383, as said below
- bump_cond: float32 [32768, 128], P(('grp', 'die')), may hold values from 0.3 to 3
- pkg_volt: float32 [16384, 128], P('die'), may hold values from -6 to 6
- pkg_diag: float32 [16384, 128], P('die'), may hold values from 4 to 6
- pkg_pattern: int32 [4, 16384], P(None, 'die'), may hold values from 0 to 16383, as said below
- pkg_weight: float32 [4, 16384], P(None, 'die'), may hold values from -0.5 to 0.5
- block_coupling: float32 [128, 128], replicated, may hold values from -0.5 to 0.5
Outputs:
- die_out: float32 [4096, 4096], P('grp', 'die')
- pkg_out: float32 [16384, 128], P('die')
- bump_out: float32 [32768, 128], P(('grp', 'die'))
Inputs may be any that keep to these rules, and one draw needn't show every extreme that they name: `bump_node`: live slots of a block come first; each block has 52 or more live slots. `bump_block`: bump block j of a device (j counted within the device) targets a package block of die shard j // 4, that is a block b with b // 1024 = j // 4. pkg_pattern[k, b] lies within 32 blocks of b.
All inputs are finite; a program needn't handle non-finite values.
Results may differ from a plain program's by a relative error of at most 0.0001.
Values sent between devices are 32-bit elements; how exact they have to be, the bound alone decides.
A program may use at most 64 MiB of HBM per device.

v0:
```python
import math

import jax
import jax.numpy as jnp
from jax import lax
from jax.sharding import PartitionSpec as P

RADIUS = 32
SWEEPS = 4
ITERS = 4


def with_halo(cells, sides, width):
    for axis, dim in sides:
        count = lax.axis_size(axis)
        ends = count - 1
        head = lax.slice_in_dim(cells, 0, width, axis=dim)
        tail = lax.slice_in_dim(cells, cells.shape[dim] - width, cells.shape[dim], axis=dim)
        cells = jnp.concatenate(
            [
                lax.ppermute(tail, axis, [(i, (i + 1) % count) for i in range(ends)]),
                cells,
                lax.ppermute(head, axis, [((i + 1) % count, i) for i in range(ends)]),
            ],
            axis=dim,
        )
    return cells


def sweep_weights(sweeps):
    return [
        1.0 / (1.0 + 0.8 * math.cos(math.pi * (2 * index + 1) / (2 * sweeps)))
        for index in range(sweeps)
    ]


def fetch_bumps(plane_shard, block_ids, plane_start):
    picked = plane_shard[
        lax.all_to_all(block_ids, "die", split_axis=0, concat_axis=0, tiled=True) - plane_start
    ]
    return lax.all_to_all(picked, "die", split_axis=0, concat_axis=0, tiled=True)


def local(
    die_volt,
    die_load,
    die_shunt,
    bump_node,
    bump_block,
    bump_cond,
    pkg_volt,
    pkg_diag,
    pkg_pattern,
    pkg_weight,
    block_coupling,
):
    die_count = lax.axis_size("die")
    blocks_dev = pkg_volt.shape[0]
    plane_start = lax.axis_index("die") * blocks_dev
    capacity = bump_block.shape[0] // die_count
    tile_rows, tile_cols = die_volt.shape
    live_slot = bump_node >= 0
    safe_node = jnp.where(live_slot, bump_node, 0).reshape(-1)
    conductance = jnp.where(live_slot, bump_cond, jnp.float32(0.0))
    block_ids = bump_block.reshape(die_count, capacity)
    bump_start = fetch_bumps(pkg_volt, block_ids, plane_start).reshape(-1, 128)
    flat_zero = jnp.zeros((tile_rows * tile_cols,), jnp.float32)
    gsum = flat_zero.at[safe_node].add(conductance.reshape(-1)).reshape(tile_rows, tile_cols)
    inject = (
        flat_zero.at[safe_node]
        .add((conductance * bump_start).reshape(-1))
        .reshape(tile_rows, tile_cols)
    )
    diagonal = 4.0 + die_shunt + gsum
    right_side = inject - die_load
    voltage = die_volt
    for weight in sweep_weights(SWEEPS):
        padded = with_halo(voltage, (("grp", 0), ("die", 1)), 1)
        beside = padded[2:, 1:-1] + padded[:-2, 1:-1] + padded[1:-1, 2:] + padded[1:-1, :-2]
        voltage = voltage + weight * (right_side - diagonal * voltage + beside) / diagonal
    at_bump = voltage.reshape(-1)[safe_node].reshape(-1, 128)
    current = (conductance * (bump_start - at_bump)).reshape(die_count, capacity, 128)
    block_code = block_ids.astype(jnp.float32)
    got_current, got_code = (
        lax.all_to_all(current, "die", split_axis=0, concat_axis=0, tiled=True),
        lax.all_to_all(block_code, "die", split_axis=0, concat_axis=0, tiled=True),
    )
    got_blocks = got_code.astype(jnp.int32)
    local_sum = (
        jnp.zeros((blocks_dev, 128), jnp.float32)
        .at[(got_blocks - plane_start).reshape(-1)]
        .add(got_current.reshape(-1, 128))
    )
    inflow = lax.psum(local_sum, "grp")
    local_index = pkg_pattern - plane_start + RADIUS
    plane = pkg_volt
    for iteration in range(ITERS):
        extended = with_halo(plane, (("die", 0),), RADIUS)
        coupled = jnp.dot(
            plane,
            block_coupling,
            precision=lax.Precision.HIGHEST,
            preferred_element_type=jnp.float32,
        )
        for neighbour in range(pkg_pattern.shape[0]):
            coupled = coupled + pkg_weight[neighbour][:, None] * extended[local_index[neighbour]]
        plane = (-inflow - coupled) / pkg_diag
    bump_out = fetch_bumps(plane, block_ids, plane_start).reshape(-1, 128)
    return (voltage, plane, bump_out)


def solution(mesh):
    return jax.shard_map(
        local,
        mesh=mesh,
        in_specs=(
            P("grp", "die"),
            P("grp", "die"),
            P("grp", "die"),
            P(("grp", "die"), None),
            P(("grp", "die")),
            P(("grp", "die"), None),
            P("die", None),
            P("die", None),
            P(None, "die"),
            P(None, "die"),
            P(),
        ),
        out_specs=(P("grp", "die"), P("die", None), P(("grp", "die"), None)),
        check_vma=False,
    )
```

profile of v0, /device:TPU:1, one launch (start us, length us, event | category | flops | bytes accessed | tf_op | source)
XLA Modules:
  0.0 650.1 jit_solution(12804207416585211754)
XLA Ops:
  9.8 11.9 %all-to-all-start.2 = ((f32[16,1,4]{2,1,0:T(1,128)}), f32[16,1,4]{2,1,0:T(1,128)S(1)}, u32[]{:S(2)}, u32[]{:S(2)}) async-start(f32[16,1,4]{2,1,0:T(1,128)} %bitcast.8), calls=%async_computation.2 | async-start | bytes 16384 | tf_op jit(solution)/shard_map/all_to_all | solution.py:86
  22.5 4.0 collective-permute-start.1
  30.5 4.2 collective-permute-start.16
  34.7 7.7 %all-to-all-start = ((s32[16,1,4]{2,1,0:T(1,128)}), s32[16,1,4]{2,1,0:T(1,128)S(1)}, u32[]{:S(2)}, u32[]{:S(2)}) async-start(s32[16,1,4]{2,1,0:T(1,128)} %bitcast.2), calls=%async_computation | async-start | bytes 16384 | tf_op jit(solution)/shard_map/all_to_all | solution.py:39
  42.4 7.2 %all-to-all-done = s32[16,1,4]{2,1,0:T(1,128)S(1)} async-done(((s32[16,1,4]{2,1,0:T(1,128)}), s32[16,1,4]{2,1,0:T(1,128)S(1)}, u32[]{:S(2)}, u32[]{:S(2)}) %all-to-all-start) | async-done | bytes 288 | tf_op jit(solution)/shard_map/all_to_all | solution.py:39
  57.2 4.0 collective-permute-start.3
  63.4 46.9 %scatter_custom_fusion.1 = f32[32768]{0:T(1024)S(1)} fusion(s32[8192]{0:T(1024)S(1)} %bitcast.63, f32[8192]{0:T(1024)S(1)} %get-tuple-element.30, f32[]{:T(128)} %constant.12.clone.1), kind=kCustom, calls=%fused_computation.97 | custom fusion | flops 8192 | bytes 131076 | tf_op jit(solution)/shard_map/scatter-add | solution.py:68
  110.3 46.9 %scatter_custom_fusion = f32[32768]{0:T(1024)S(1)} fusion(s32[8192]{0:T(1024)S(1)} %bitcast.64, f32[8192]{0:T(1024)S(1)} %get-tuple-element.31, f32[]{:T(128)} %constant.12.clone.1), kind=kCustom, calls=%fused_computation.99 | custom fusion | flops 8192 | bytes 131076 | tf_op jit(solution)/shard_map/scatter-add | solution.py:71
  158.4 5.9 collective-permute-start.5
  185.7 4.6 collective-permute-start.11
  201.1 4.6 collective-permute-start.15
  207.9 45.5 %gather_fusion.1 = f32[8192]{0:T(1024)S(1)} fusion(f32[32768]{0:T(1024)S(1)} %bitcast.58, s32[8192]{0:T(1024)S(1)} %broadcast_clamp_fusion), kind=kCustom, calls=%fused_computation.1 | custom fusion | bytes 98304 | tf_op jit(solution)/shard_map/gather | solution.py:81
  254.1 12.6 %all-to-all-start.3 = ((f32[16,4,128]{2,1,0:T(4,128)}), f32[16,4,128]{2,1,0:T(4,128)S(1)}, u32[]{:S(2)}, u32[]{:S(2)}) async-start(f32[16,4,128]{2,1,0:T(4,128)} %bitcast.11), calls=%async_computation.3 | async-start | bytes 65536 | tf_op jit(solution)/shard_map/all_to_all | solution.py:85
  266.7 7.3 %all-to-all-done.3 = f32[16,4,128]{2,1,0:T(4,128)S(1)} async-done(((f32[16,4,128]{2,1,0:T(4,128)}), f32[16,4,128]{2,1,0:T(4,128)S(1)}, u32[]{:S(2)}, u32[]{:S(2)}) %all-to-all-start.3) | async-done | bytes 32800 | tf_op jit(solution)/shard_map/all_to_all | solution.py:85
  284.2 4.0 gather_fusion.2
  288.3 267.0 %all-reduce.2.cloned.1.call-done = f32[1024,128]{1,0:T(8,128)} async-done(((f32[1024,128]{1,0:T(8,128)}), f32[1024,128]{1,0:T(8,128)}) %all-reduce.2.cloned.1.call-update) | async-done | bytes 524304 | tf_op jit(solution)/shard_map/psum | solution.py:94
  570.7 4.0 gather_fusion.7
  574.7 4.0 gather_fusion.6
  595.1 4.0 gather_fusion.11
  599.2 4.0 gather_fusion.10
  605.2 4.6 collective-permute-start.22
  619.9 4.0 gather_fusion.15
  623.9 4.0 gather_fusion.14
  630.5 12.1 %all_to_all.31 = f32[16,4,128]{2,1,0:T(4,128)S(1)} all-to-all(f32[16,4,128]{2,1,0:T(4,128)S(1)} %bitcast.62), channel_id=1, replica_groups=mesh['grp'=32,'die'=16] {'die'}, dimensions={0} | all-to-all | bytes 65536 | tf_op jit(solution)/shard_map/all_to_all | solution.py:41
  (142 shorter events, 110.0 us)
Async XLA Ops:
  9.8 24.8 %all-to-all-start.2 = ((f32[16,1,4]{2,1,0:T(1,128)}), f32[16,1,4]{2,1,0:T(1,128)S(1)}, u32[]{:S(2)}, u32[]{:S(2)}) async-start(f32[16,1,4]{2,1,0:T(1,128)} %bitcast.8), calls=%async_computation.2 | async-start | bytes 16384 | tf_op jit(solution)/shard_map/all_to_all | solution.py:86
  22.5 33.3 %collective-permute-start.1 = (f32[1,256]{1,0:T(1,128)S(1)}, f32[1,256]{1,0:T(1,128)S(1)}, u32[]{:S(2)}, u32[]{:S(2)}) collective-permute-start(f32[1,256]{1,0:T(1,128)S(1)} %get-tuple-element.28), channel_id=1, source_target_pairs={{0,16},{16,32},{32,48},{48,64},{64,80},{80,96},{96,112},{112,128},... | collective-permute-start | bytes 3080 | tf_op jit(solution)/shard_map/ppermute | solution.py:21
  26.5 29.2 %collective-permute-start = (f32[1,256]{1,0:T(1,128)S(1)}, f32[1,256]{1,0:T(1,128)S(1)}, u32[]{:S(2)}, u32[]{:S(2)}) collective-permute-start(f32[1,256]{1,0:T(1,128)S(1)} %get-tuple-element.29), channel_id=1, source_target_pairs={{16,0},{32,16},{48,32},{64,48},{80,64},{96,80},{112,96},{128,112},... | collective-permute-start | bytes 3080 | tf_op jit(solution)/shard_map/ppermute | solution.py:23
  29.2 246.6 %collective-permute-start.17 = (f32[32,128]{1,0:T(8,128)S(1)}, f32[32,128]{1,0:T(8,128)S(1)}, u32[]{:S(2)}, u32[]{:S(2)}) collective-permute-start(f32[32,128]{1,0:T(8,128)S(1)} %get-tuple-element.12), channel_id=1, source_target_pairs={{1,0},{2,1},{3,2},{4,3},{5,4},{6,5},{7,6},{8,7},{9,8},{10,9},{11,1... | collective-permute-start | bytes 49160 | tf_op jit(solution)/shard_map/ppermute | solution.py:23
  30.5 245.2 %collective-permute-start.16 = (f32[32,128]{1,0:T(8,128)S(1)}, f32[32,128]{1,0:T(8,128)S(1)}, u32[]{:S(2)}, u32[]{:S(2)}) collective-permute-start(f32[32,128]{1,0:T(8,128)S(1)} %get-tuple-element.13), channel_id=1, source_target_pairs={{0,1},{1,2},{2,3},{3,4},{4,5},{5,6},{6,7},{7,8},{8,9},{9,10},{10,1... | collective-permute-start | bytes 49160 | tf_op jit(solution)/shard_map/ppermute | solution.py:21
  34.7 14.9 %all-to-all-start = ((s32[16,1,4]{2,1,0:T(1,128)}), s32[16,1,4]{2,1,0:T(1,128)S(1)}, u32[]{:S(2)}, u32[]{:S(2)}) async-start(s32[16,1,4]{2,1,0:T(1,128)} %bitcast.2), calls=%async_computation | async-start | bytes 16384 | tf_op jit(solution)/shard_map/all_to_all | solution.py:39
  52.2 11.1 %all-to-all-start.1 = ((f32[16,4,128]{2,1,0:T(4,128)}), f32[16,4,128]{2,1,0:T(4,128)S(1)}, u32[]{:S(2)}, u32[]{:S(2)}) async-start(f32[16,4,128]{2,1,0:T(4,128)} %bitcast.4), calls=%async_computation.1 | async-start | bytes 65536 | tf_op jit(solution)/shard_map/all_to_all | solution.py:41
  55.9 101.5 %collective-permute-start.2 = (f32[130,1]{1,0:T(8,128)S(1)}, f32[130,1]{1,0:T(8,128)S(1)}, u32[]{:S(2)}, u32[]{:S(2)}) collective-permute-start(f32[130,1]{1,0:T(8,128)S(1)} %get-tuple-element.20), channel_id=1, source_target_pairs={{1,0},{2,1},{3,2},{4,3},{5,4},{6,5},{7,6},{8,7},{9,8},{10,9},{11,1... | collective-permute-start | bytes 1568 | tf_op jit(solution)/shard_map/ppermute | solution.py:23
  57.2 100.2 %collective-permute-start.3 = (f32[130,1]{1,0:T(8,128)S(1)}, f32[130,1]{1,0:T(8,128)S(1)}, u32[]{:S(2)}, u32[]{:S(2)}) collective-permute-start(f32[130,1]{1,0:T(8,128)S(1)} %get-tuple-element.21), channel_id=1, source_target_pairs={{0,1},{1,2},{2,3},{3,4},{4,5},{5,6},{6,7},{7,8},{8,9},{9,10},{10,1... | collective-permute-start | bytes 1568 | tf_op jit(solution)/shard_map/ppermute | solution.py:21
  158.4 8.4 %collective-permute-start.5 = (f32[1,256]{1,0:T(1,128)S(1)}, f32[1,256]{1,0:T(1,128)S(1)}, u32[]{:S(2)}, u32[]{:S(2)}) collective-permute-start(f32[1,256]{1,0:T(1,128)S(1)} %get-tuple-element.26), channel_id=1, source_target_pairs={{0,16},{16,32},{32,48},{48,64},{64,80},{80,96},{96,112},{112,128},... | collective-permute-start | bytes 3080 | tf_op jit(solution)/shard_map/ppermute | solution.py:21
  169.3 5.3 collective-permute-start.6
  170.6 5.3 collective-permute-start.7
  176.2 5.2 collective-permute-start.9
  184.4 6.0 collective-permute-start.10
  185.7 6.0 collective-permute-start.11
  191.9 4.9 collective-permute-start.13
  199.8 6.0 collective-permute-start.14
  201.1 6.0 collective-permute-start.15
  254.1 19.9 %all-to-all-start.3 = ((f32[16,4,128]{2,1,0:T(4,128)}), f32[16,4,128]{2,1,0:T(4,128)S(1)}, u32[]{:S(2)}, u32[]{:S(2)}) async-start(f32[16,4,128]{2,1,0:T(4,128)} %bitcast.11), calls=%async_computation.3 | async-start | bytes 65536 | tf_op jit(solution)/shard_map/all_to_all | solution.py:85
  266.7 288.6 %all-reduce.2.cloned.1.call-start = ((), (), s32[]{:S(2)}) async-start(), calls=%async_computation.5 | async-start | bytes 1048576 | tf_op jit(solution)/shard_map/psum | solution.py:94
  557.2 5.2 collective-permute-start.18
  580.7 5.3 collective-permute-start.20
  583.9 5.5 collective-permute-start.21
  605.2 6.5 collective-permute-start.22
  (18 other events, 514.6 us)
Sparse Core Ops, SparseCore 0:
  275.8 279.4 all-reduce.1
where the time goes:
time: 655 us; the launch traced here: 650 us
  waiting for transfers between devices  305 us (47%)
  local copies, waits for them, and re-layouts  108 us (16%)
  other arithmetic  106 us (16%)
  starting transfers between devices  102 us (16%)
  between operations  14.9 us (2%)
  blocking collectives  12.1 us (2%)
    psum x1, waiting for transfers between devices, local(): inflow = lax.psum(local_sum, 'grp')  267 us
    gather x16, local copies, waits for them, and re-layouts, local(): extended[local_index[neighbour]]  53.5 us
    ppermute x12, starting transfers between devices, with_halo(): lax.ppermute(tail, axis, [(i, (i + 1) % count) for i in range(ends)])  48.6 us
    scatter-add x1, other arithmetic, local(): flat_zero.at[safe_node].add(conductance.reshape(-1))  46.9 us
    scatter-add x1, other arithmetic, local(): inject = flat_zero.at[safe_node].add((conductance * bump_start).reshape(-...  46.9 us
    gather x1, local copies, waits for them, and re-layouts, local(): at_bump = voltage.reshape(-1)[safe_node].reshape(-1, 128)  45.5 us
    ppermute x12, starting transfers between devices, with_halo(): lax.ppermute(head, axis, [((i + 1) % count, i) for i in range(ends)])  18.2 us
    ppermute x12, waiting for transfers between devices, with_halo(): lax.ppermute(head, axis, [((i + 1) % count, i) for i in range(ends)])  16.9 us
  transfers between devices with their start and end apart: 29, of which 13 were waited for; matrix products, arithmetic and copies ran while one was open for 25% of the time, Pallas kernels for 0%

commit v1 on v0

v1 whole, which is shorter than its diff:
```python
import functools
import math

import jax
import jax.numpy as jnp
from jax import lax
from jax.experimental import pallas as pl
from jax.experimental.pallas import tpu as pltpu
from jax.sharding import PartitionSpec as P

SWEEPS = 4
ITERS = 4
MESH = pl.DeviceIdType.MESH
F32 = jnp.float32
BF16 = jnp.bfloat16


def sweep_weights(sweeps):
    return [
        1.0 / (1.0 + 0.8 * math.cos(math.pi * (2 * index + 1) / (2 * sweeps)))
        for index in range(sweeps)
    ]


def split(x):
    hi = x.astype(BF16)
    lo = (x - hi.astype(F32)).astype(BF16)
    return hi, lo


def remote(src, dst, send_sem, recv_sem, **device):
    return pltpu.make_async_remote_copy(
        src_ref=src,
        dst_ref=dst,
        send_sem=send_sem,
        recv_sem=recv_sem,
        device_id=device,
        device_id_type=MESH,
    )


def signal(barrier, **device):
    pl.semaphore_signal(barrier, inc=1, device_id=device, device_id_type=MESH)


def pick_rows(ids, first, planes, into):
    lane = lax.broadcasted_iota(jnp.int32, ids.shape, 1) + first
    into[...] = jnp.zeros_like(into)

    def step(c, carry):
        start = pl.multiple_of(c * 256, 256)
        onehot = jnp.concatenate(
            [
                jnp.where(ids == lane + (start + part), 1.0, 0.0).astype(BF16)
                for part in (0, 128)
            ],
            axis=1,
        )
        both = jnp.dot(onehot, planes[pl.ds(start, 256), :], preferred_element_type=F32)
        into[...] += both[:, :128] + both[:, 128:]
        return carry

    lax.fori_loop(0, planes.shape[0] // 256, step, 0)


class Exchange:
    def __init__(self, count, me, src, dst, send_sem, recv_sem):
        self.count, self.me = count, me
        self.src, self.dst = src, dst
        self.send_sem, self.recv_sem = send_sem, recv_sem

    def copy(self, k):
        to = lax.rem(self.me + k, self.count)
        return remote(
            self.src.at[to],
            self.dst.at[self.me],
            self.send_sem.at[k],
            self.recv_sem.at[k],
            die=to,
        )

    def start(self):
        for k in range(1, self.count):
            self.copy(k).start()
        self.dst[self.me] = self.src[self.me]

    def wait(self):
        for k in range(1, self.count):
            self.copy(k).wait_recv()

    def drain(self):
        for k in range(1, self.count):
            self.copy(k).wait_send()


def die_kernel(
    nd, ng, cap, blocks,
    volt_ref, load_ref, shunt_ref, node_ref, ids_ref, cond_ref, pkg_ref,
    out_ref, item_ref, rids_ref,
    ids_got, rows_out, rows_got, cur_out, cur_got,
    start_ref, planes, onecol, acc, vx, rx, dx, edge_n, edge_s, edge_w, edge_e,
    halo_n, halo_s, halo_w, halo_e, halo_nw, halo_ne, halo_sw, halo_se,
    sem_ids, sem_rows, sem_cur, sem_halo,
):
    me, mg = lax.axis_index("die"), lax.axis_index("grp")
    rows, cols = volt_ref.shape
    nblk = node_ref.shape[0]
    up, down = lax.rem(mg + ng - 1, ng), lax.rem(mg + 1, ng)
    west, east = lax.rem(me + nd - 1, nd), lax.rem(me + 1, nd)
    barrier = pltpu.get_barrier_semaphore()
    for k in range(1, nd):
        signal(barrier, die=lax.rem(me + k, nd))
    for g in (up, down):
        for d in (west, me, east):
            signal(barrier, grp=g, die=d)

    chunk = 8
    steps = nblk // chunk

    def one_columns(it, carry):
        node = node_ref[pl.ds(pl.multiple_of(it * chunk, chunk), chunk), :]
        col = jnp.bitwise_and(node, cols - 1)
        for i in range(chunk):
            iota = lax.broadcasted_iota(jnp.int32, (cols, 128), 0)
            onecol[it * chunk + i] = jnp.where(iota == col[i : i + 1, :], 1.0, 0.0).astype(BF16)
        return carry

    lax.fori_loop(0, steps, one_columns, 0)
    pl.semaphore_wait(barrier, nd - 1 + 6)

    ids = Exchange(nd, me, ids_ref, ids_got, sem_ids.at[0], sem_ids.at[1])
    ids.start()

    row_iota = lax.broadcasted_iota(jnp.int32, (rows, 128), 0)

    def scatter(value_of, slot):
        def step(it, carry):
            at = pl.ds(pl.multiple_of(it * chunk, chunk), chunk)
            node = node_ref[at, :]
            row = jnp.right_shift(node, cols.bit_length() - 1)
            hi, lo = [v.astype(F32) for v in split(value_of(at))]
            parts_hi, parts_lo = [], []
            for i in range(chunk):
                here = row_iota == row[i : i + 1, :]
                parts_hi.append(jnp.where(here, hi[i : i + 1, :], 0.0).astype(BF16))
                parts_lo.append(jnp.where(here, lo[i : i + 1, :], 0.0).astype(BF16))
            left = jnp.concatenate(
                [jnp.concatenate(parts_hi, axis=1), jnp.concatenate(parts_lo, axis=1)], axis=0
            )
            right = jnp.concatenate([onecol[it * chunk + i] for i in range(chunk)], axis=1)
            both = lax.dot_general(
                left, right, (((1,), (1,)), ((), ())), preferred_element_type=F32
            )
            acc[slot] += both[:rows] + both[rows:]
            return carry

        acc[slot] = jnp.zeros((rows, cols), F32)
        lax.fori_loop(0, steps, step, 0)

    scatter(lambda at: jnp.where(node_ref[at, :] >= 0, cond_ref[at, :], 0.0), 0)
    inverse = 1.0 / (4.0 + shunt_ref[...] + acc[0])

    ids.wait()
    wanted = jnp.concatenate([ids_got[j] for j in range(nd)], axis=0)
    rids_ref[...] = wanted
    planes[...] = jnp.concatenate(split(pkg_ref[...]), axis=1)
    pick_rows(wanted, me * blocks, planes, start_ref)
    for j in range(nd):
        rows_out[j] = start_ref[j * cap : (j + 1) * cap, :]
    rows_x = Exchange(nd, me, rows_out, rows_got, sem_rows.at[0], sem_rows.at[1])
    rows_x.start()

    lane = lax.broadcasted_iota(jnp.int32, (nblk, 128), 1)
    sub = lax.broadcasted_iota(jnp.int32, (nblk, 128), 0)
    mine = jnp.logical_or(lane == sub, lane == sub + 64)
    in_lanes = jnp.sum(jnp.where(mine, wanted.astype(F32), 0.0), axis=0, keepdims=True)

    rows_x.wait()
    for j in range(nd):
        start_ref[j * cap : (j + 1) * cap, :] = rows_got[j]
    scatter(
        lambda at: jnp.where(node_ref[at, :] >= 0, cond_ref[at, :] * start_ref[at, :], 0.0), 1
    )
    right_side = acc[1] - load_ref[...]

    middle = (slice(8, 8 + rows), slice(128, 128 + cols))
    for k, (ext, tile) in enumerate(
        ((vx, volt_ref[...]), (rx, right_side), (dx, inverse))
    ):
        ext[middle] = tile
        for b in range(2):
            side = slice(b * (cols - 128), b * (cols - 128) + 128)
            edge_n[b, 8 * k : 8 * k + 8, :] = tile[:8, side]
            edge_s[b, 8 * k : 8 * k + 8, :] = tile[rows - 8 :, side]
        edge_w[8 * k : 8 * k + 8, :] = jnp.transpose(tile[:, :128])[:8]
        edge_e[8 * k : 8 * k + 8, :] = jnp.transpose(tile[:, cols - 128 :])[120:]
    halos = [
        remote(src, dst, sem_halo.at[0, k], sem_halo.at[1, k], grp=g, die=d)
        for k, (src, dst, g, d) in enumerate(
            (
                (edge_n, halo_s, up, me),
                (edge_s, halo_n, down, me),
                (edge_w, halo_e, mg, west),
                (edge_e, halo_w, mg, east),
                (edge_n.at[0], halo_se, up, west),
                (edge_n.at[1], halo_sw, up, east),
                (edge_s.at[0], halo_ne, down, west),
                (edge_s.at[1], halo_nw, down, east),
            )
        )
    ]
    for copy in halos:
        copy.start()
    for copy in halos:
        copy.wait_recv()
    pad = jnp.zeros((120, 128), F32)
    for k, ext in enumerate((vx, rx, dx)):
        at = slice(8 * k, 8 * k + 8)
        for b in range(2):
            side = slice(128 + b * (cols - 128), 256 + b * (cols - 128))
            ext[0:8, side] = halo_n[b, at, :]
            ext[8 + rows :, side] = halo_s[b, at, :]
        ext[8 : 8 + rows, 0:128] = jnp.transpose(jnp.concatenate([pad, halo_w[at, :]], axis=0))
        ext[8 : 8 + rows, 128 + cols :] = jnp.transpose(
            jnp.concatenate([halo_e[at, :], pad], axis=0)
        )
        ext[0:8, 0:128] = halo_nw[at, :]
        ext[0:8, 128 + cols :] = halo_ne[at, :]
        ext[8 + rows :, 0:128] = halo_sw[at, :]
        ext[8 + rows :, 128 + cols :] = halo_se[at, :]

    height, width = rows + 16, cols + 256
    grow = lax.broadcasted_iota(jnp.int32, (height, width), 0) + (mg * rows - 8)
    gcol = lax.broadcasted_iota(jnp.int32, (height, width), 1) + (me * cols - 128)
    inside = (grow >= 0) & (grow < ng * rows) & (gcol >= 0) & (gcol < nd * cols)
    v = jnp.where(inside, vx[...], 0.0)
    r = rx[...]
    inv = dx[...]
    for weight in sweep_weights(SWEEPS):
        beside = (
            pltpu.roll(v, 1, 0)
            + pltpu.roll(v, height - 1, 0)
            + pltpu.roll(v, 1, 1)
            + pltpu.roll(v, width - 1, 1)
        )
        v = jnp.where(inside, v + weight * ((r + beside) * inv - v), 0.0)
    final = v[middle]
    out_ref[...] = final
    halves = jnp.concatenate(split(final), axis=0)

    def currents(it, carry):
        at = pl.ds(pl.multiple_of(it * chunk, chunk), chunk)
        node = node_ref[at, :]
        row = jnp.right_shift(node, cols.bit_length() - 1)
        right = jnp.concatenate([onecol[it * chunk + i] for i in range(chunk)], axis=1)
        both = jnp.dot(halves, right, preferred_element_type=F32)
        by_row = both[:rows] + both[rows:]
        seen = [
            jnp.sum(
                jnp.where(row_iota == row[i : i + 1, :], by_row[:, 128 * i : 128 * i + 128], 0.0),
                axis=0,
                keepdims=True,
            )
            for i in range(chunk)
        ]
        flow = jnp.where(
            node >= 0, cond_ref[at, :] * (start_ref[at, :] - jnp.concatenate(seen, axis=0)), 0.0
        )
        for i in range(chunk // cap):
            cur_out[it * (chunk // cap) + i] = flow[i * cap : (i + 1) * cap]
        return carry

    lax.fori_loop(0, steps, currents, 0)
    cur_x = Exchange(nd, me, cur_out, cur_got, sem_cur.at[0], sem_cur.at[1])
    cur_x.start()
    cur_x.wait()
    for j in range(nd):
        item_ref[j * cap : (j + 1) * cap, :] = cur_got[j]
    item_ref[nblk:, :] = jnp.broadcast_to(in_lanes, (8, 128))
    for x in (ids, rows_x, cur_x):
        x.drain()
    for copy in halos:
        copy.wait_send()


def pkg_kernel(
    nd, ng, cap, blocks,
    item_ref, rids_ref, pkg_ref, diag_ref, pat_ref, wt_ref, coup_ref,
    plane_ref, bump_ref,
    items, x_f, x_s, inf_x, diag_x, pat_x, wt_x, wmat, acc, rows_out, rows_got,
    sem_const, sem_ring, sem_ring_send, sem_part, sem_core, sem_core_send, sem_inf, sem_rows,
):
    me, mg = lax.axis_index("die"), lax.axis_index("grp")
    ny = ng // 4
    half = ny // 2
    c = lax.rem(mg, 2)
    y = lax.rem(mg // 2, ny)
    h = mg // (2 * ny)
    nblk = rids_ref.shape[0]
    ext = blocks + 256
    tiles = ext // 128

    def index(hh, yy, cc):
        return (hh * ny + yy) * 2 + cc

    plus, minus = lax.rem(y + 1, ny), lax.rem(y + ny - 1, ny)
    west, east = lax.rem(me + nd - 1, nd), lax.rem(me + 1, nd)
    barrier = pltpu.get_barrier_semaphore()
    for k in range(1, nd):
        signal(barrier, die=lax.rem(me + k, nd))
    for g in (index(h, plus, c), index(h, minus, c), index(1 - h, y, c), index(h, y, 1 - c)):
        signal(barrier, grp=g)

    own = pl.ds(128, blocks)
    diag_x[own, :] = 1.0 / diag_ref[...]
    pat_x[:, 128 : 128 + blocks] = pat_ref[...]
    wt_x[:, 128 : 128 + blocks] = wt_ref[...]
    for ref in (x_s,):
        ref[0:64, :] = jnp.zeros((64, 256), BF16)
        ref[64 + ext :, :] = jnp.zeros((64, 256), BF16)
    inf_x[0:32, :] = jnp.zeros((32, 128), F32)
    inf_x[ext - 32 :, :] = jnp.zeros((32, 128), F32)
    items[mg] = item_ref[...]

    def build(t, carry):
        at = pl.ds(pl.multiple_of(t * 128, 128), 128)
        ids = pat_x[:, at] + (128 + 64 - me * blocks - t * 128)
        weights = wt_x[:, at]
        source = lax.broadcasted_iota(jnp.int32, (256, 128), 0)
        total = jnp.zeros((256, 128), F32)
        for k in range(ids.shape[0]):
            total += jnp.where(source == ids[k : k + 1, :], weights[k : k + 1, :], 0.0)
        wmat[t] = jnp.concatenate(split(jnp.transpose(total)), axis=0)
        return carry

    lax.fori_loop(1, tiles - 1, build, 0)
    pl.semaphore_wait(barrier, nd - 1 + 4)

    tail, head = pl.ds(128 + blocks, 128), pl.ds(0, 128)
    first, last = pl.ds(0, 128), pl.ds(blocks - 128, 128)
    lanes_tail, lanes_last = slice(128 + blocks, 256 + blocks), slice(blocks - 128, blocks)

    core = index(h, y, 1 - c)
    part = index(1 - h, y, c)
    right, left = index(h, plus, c), index(h, minus, c)

    def held(dist, k):
        hh = h if k == 0 else 1 - h
        return index(hh, lax.rem(y + ny + dist, ny), c)

    def pass_on(slot, to, direction, dist, k):
        copy = remote(
            items.at[slot],
            items.at[slot],
            sem_ring_send.at[direction, dist, k],
            sem_ring.at[direction, dist, k],
            grp=to,
        )
        copy.start()
        return copy

    def ring_wait(direction, dist, k):
        slot = held(-dist if direction == 0 else dist, k)
        remote(
            items.at[slot],
            items.at[slot],
            sem_ring_send.at[direction, dist, k],
            sem_ring.at[direction, dist, k],
            grp=right if direction == 0 else left,
        ).wait_recv()
        return slot

    sent = []
    core_sent = []

    def to_core(slot):
        n = len(core_sent)
        copy = remote(
            items.at[slot], items.at[slot], sem_core_send.at[n], sem_core.at[n], grp=core
        )
        copy.start()
        core_sent.append(copy)

    reach = {(0, 0): half, (0, 1): half - 1, (1, 0): half - 1, (1, 1): half}
    for direction, to in ((0, right), (1, left)):
        if reach[direction, 0] >= 1:
            sent.append(pass_on(mg, to, direction, 1, 0))
    to_part = remote(items.at[mg], items.at[mg], sem_part.at[0], sem_part.at[1], grp=part)
    to_part.start()
    to_core(mg)
    consts = []
    for k, (src, dst) in enumerate(
        (
            (pkg_ref.at[first], x_f.at[tail]),
            (diag_x.at[pl.ds(128, 128)], diag_x.at[tail]),
            (pat_ref.at[:, 0:128], pat_x.at[:, lanes_tail]),
            (wt_ref.at[:, 0:128], wt_x.at[:, lanes_tail]),
        )
    ):
        consts.append(remote(src, dst, sem_const.at[0, k], sem_const.at[1, k], die=west))
    for k, (src, dst) in enumerate(
        (
            (pkg_ref.at[last], x_f.at[head]),
            (diag_x.at[pl.ds(blocks, 128)], diag_x.at[head]),
            (pat_ref.at[:, lanes_last], pat_x.at[:, 0:128]),
            (wt_ref.at[:, lanes_last], wt_x.at[:, 0:128]),
        )
    ):
        consts.append(remote(src, dst, sem_const.at[0, 4 + k], sem_const.at[1, 4 + k], die=east))
    for copy in consts:
        copy.start()
    to_part.wait_recv()
    for direction, to in ((0, right), (1, left)):
        if reach[direction, 1] >= 1:
            sent.append(pass_on(part, to, direction, 1, 1))
    to_core(part)
    for dist in range(1, half + 1):
        for k in range(2):
            for direction, to in ((0, right), (1, left)):
                if reach[direction, k] >= dist:
                    slot = ring_wait(direction, dist, k)
                    if reach[direction, k] >= dist + 1:
                        sent.append(pass_on(slot, to, direction, dist + 1, k))
                    to_core(slot)

    for copy in consts:
        copy.wait_recv()
    lax.fori_loop(0, 2, lambda i, carry: build(i * (tiles - 1), carry), 0)
    x_s[64 : 64 + 128, :] = jnp.concatenate(split(x_f[0:128, :]), axis=1)
    x_s[64 + 128 : 64 + 128 + blocks, :] = jnp.concatenate(split(pkg_ref[...]), axis=1)
    x_s[64 + 128 + blocks : 64 + ext, :] = jnp.concatenate(split(x_f[128 + blocks :, :]), axis=1)
    for copy in core_sent:
        copy.wait_recv()

    lane = lax.broadcasted_iota(jnp.int32, (1, 128), 1)
    acc[...] = jnp.zeros((blocks, 256), F32)
    pairs = nblk * 2 == 128

    def gather_sum(q, carry):
        target = lax.broadcasted_iota(jnp.int32, (blocks, 128), 0) + me * blocks
        ones, values = [], []
        for p in range(2):
            a, b = items[4 * q + 2 * p], items[4 * q + 2 * p + 1]
            if pairs:
                ids = jnp.where(lane < 64, a[nblk : nblk + 1, :], b[nblk : nblk + 1, :])
                flows = (a[:nblk], b[:nblk])
            else:
                blank = jnp.zeros((64 - nblk, 128), F32)
                ids = jnp.where(lane < 64, a[nblk : nblk + 1, :], b[nblk : nblk + 1, :])
                flows = (a[:nblk], blank, b[:nblk], blank)
            ids = ids.astype(jnp.int32)
            ones.append(jnp.where(target == ids, 1.0, 0.0).astype(BF16))
            values.append(jnp.concatenate(flows, axis=0))
        acc[...] += jnp.dot(
            jnp.concatenate(ones, axis=1),
            jnp.concatenate(split(jnp.concatenate(values, axis=0)), axis=1),
            preferred_element_type=F32,
        )
        return carry

    lax.fori_loop(0, ng // 4, gather_sum, 0)
    inf_x[own, :] = acc[:, :128] + acc[:, 128:]
    infs = [
        remote(
            inf_x.at[pl.ds(128, 96)],
            inf_x.at[pl.ds(128 + blocks, 96)],
            sem_inf.at[0, 0],
            sem_inf.at[1, 0],
            die=west,
        ),
        remote(
            inf_x.at[pl.ds(32 + blocks, 96)],
            inf_x.at[pl.ds(32, 96)],
            sem_inf.at[0, 1],
            sem_inf.at[1, 1],
            die=east,
        ),
    ]
    for copy in infs:
        copy.start()
    coup = jnp.concatenate(split(coup_ref[...]), axis=1)
    for copy in infs:
        copy.wait_recv()

    for iteration in range(ITERS):
        lo_t, hi_t = (0, tiles) if iteration < ITERS - 1 else (1, tiles - 1)

        def tile(t, carry):
            start = pl.multiple_of(t * 128, 128)
            near = jnp.dot(wmat[t], x_s[pl.ds(start, 256), :], preferred_element_type=F32)
            here = x_s[pl.ds(start + 64, 128), :]
            both = jnp.concatenate([here[:, :128], here[:, 128:]], axis=0)
            block = jnp.dot(both, coup, preferred_element_type=F32)
            total = near + block
            total = total[:128] + total[128:]
            coupled = total[:, :128] + total[:, 128:]
            at = pl.ds(start, 128)
            x_f[at, :] = (-inf_x[at, :] - coupled) * diag_x[at, :]
            return carry

        lax.fori_loop(lo_t, hi_t, tile, 0)
        x_s[64 : 64 + ext, :] = jnp.concatenate(split(x_f[...]), axis=1)

    plane_ref[...] = x_f[own, :]
    pick_rows(
        rids_ref[...], me * blocks, x_s.at[pl.ds(64 + 128, blocks)], bump_ref
    )
    for j in range(nd):
        rows_out[j] = bump_ref[j * cap : (j + 1) * cap, :]
    rows_x = Exchange(nd, me, rows_out, rows_got, sem_rows.at[0], sem_rows.at[1])
    rows_x.start()
    rows_x.wait()
    for j in range(nd):
        bump_ref[j * cap : (j + 1) * cap, :] = rows_got[j]
    rows_x.drain()
    for copy in sent + core_sent + [to_part] + consts + infs:
        copy.wait_send()


def local(
    nd, ng,
    die_volt, die_load, die_shunt, bump_node, bump_block, bump_cond,
    pkg_volt, pkg_diag, pkg_pattern, pkg_weight, block_coupling,
):
    nblk = bump_node.shape[0]
    cap = nblk // nd
    blocks = pkg_volt.shape[0]
    rows, cols = die_volt.shape
    ext = blocks + 256
    vmem = pl.BlockSpec(memory_space=pltpu.VMEM)
    dma = pltpu.SemaphoreType.DMA
    ids = jnp.broadcast_to(bump_block.reshape(nd, cap, 1), (nd, cap, 128))
    exchange_f = pltpu.VMEM((nd, cap, 128), F32)
    strip = pltpu.VMEM((24, 128), F32)
    strips = pltpu.VMEM((2, 24, 128), F32)
    wide = pltpu.VMEM((rows + 16, cols + 256), F32)
    die_out, item, rids = pl.pallas_call(
        functools.partial(die_kernel, nd, ng, cap, blocks),
        out_shape=(
            jax.ShapeDtypeStruct((rows, cols), F32),
            jax.ShapeDtypeStruct((nblk + 8, 128), F32),
            jax.ShapeDtypeStruct((nblk, 128), jnp.int32),
        ),
        in_specs=[vmem] * 7,
        out_specs=(vmem,) * 3,
        scratch_shapes=[
            pltpu.VMEM((nd, cap, 128), jnp.int32),
            exchange_f, exchange_f, exchange_f, exchange_f,
            pltpu.VMEM((nblk, 128), F32),
            pltpu.VMEM((blocks, 256), BF16),
            pltpu.VMEM((nblk, cols, 128), BF16),
            pltpu.VMEM((2, rows, cols), F32),
            wide, wide, wide,
            strips, strips, strip, strip,
            strips, strips, strip, strip, strip, strip, strip, strip,
            dma((2, nd)), dma((2, nd)), dma((2, nd)), dma((2, 8)),
        ],
        compiler_params=pltpu.CompilerParams(collective_id=0, has_side_effects=True),
        name="die_round",
    )(die_volt, die_load, die_shunt, bump_node, ids, bump_cond, pkg_volt)
    plane, bump_out = pl.pallas_call(
        functools.partial(pkg_kernel, nd, ng, cap, blocks),
        out_shape=(
            jax.ShapeDtypeStruct((blocks, 128), F32),
            jax.ShapeDtypeStruct((nblk, 128), F32),
        ),
        in_specs=[vmem] * 7,
        out_specs=(vmem,) * 2,
        scratch_shapes=[
            pltpu.VMEM((ng, nblk + 8, 128), F32),
            pltpu.VMEM((ext, 128), F32),
            pltpu.VMEM((ext + 128, 256), BF16),
            pltpu.VMEM((ext, 128), F32),
            pltpu.VMEM((ext, 128), F32),
            pltpu.VMEM((pkg_pattern.shape[0], ext), jnp.int32),
            pltpu.VMEM((pkg_pattern.shape[0], ext), F32),
            pltpu.VMEM((ext // 128, 256, 256), BF16),
            pltpu.VMEM((blocks, 256), F32),
            exchange_f, exchange_f,
            dma((2, 8)),
            dma((2, ng // 8 + 2, 2)),
            dma((2, ng // 8 + 2, 2)),
            dma((2,)),
            dma((ng // 2,)),
            dma((ng // 2,)),
            dma((2, 2)),
            dma((2, nd)),
        ],
        compiler_params=pltpu.CompilerParams(collective_id=1, has_side_effects=True),
        name="package_round",
    )(item, rids, pkg_volt, pkg_diag, pkg_pattern, pkg_weight, block_coupling)
    return die_out, plane, bump_out


def solution(mesh):
    return jax.shard_map(
        functools.partial(local, mesh.shape["die"], mesh.shape["grp"]),
        mesh=mesh,
        in_specs=(
            P("grp", "die"),
            P("grp", "die"),
            P("grp", "die"),
            P(("grp", "die"), None),
            P(("grp", "die")),
            P(("grp", "die"), None),
            P("die", None),
            P("die", None),
            P(None, "die"),
            P(None, "die"),
            P(),
        ),
        out_specs=(P("grp", "die"), P("die", None), P(("grp", "die"), None)),
        check_vma=False,
    )
```

time: 655 us -> 96.2 us (0.15)
  waiting for transfers between devices: 305 us -> 0 us
  other arithmetic: 106 us -> 0 us
  local copies, waits for them, and re-layouts: 108 us -> 4.6 us
  starting transfers between devices: 102 us -> 0 us
  Pallas kernels: 0 us -> 90.7 us
  between operations: 14.9 us -> 0.66 us
  blocking collectives: 12.1 us -> 0 us
    psum x1 -> x0, waiting for transfers between devices: 267 us -> none  [local(): inflow = lax.psum(local_sum, 'grp')]
    gather x19 -> x0, local copies, waits for them, and re-layouts: 102 us -> none  [the longest x16 53.5 us: local(): extended[local_index[neighbour]]]
    scatter-add x3 -> x0, other arithmetic: 95.4 us -> none  [the longest x1 46.9 us: local(): flat_zero.at[safe_node].add(conductance.reshape(-1))]
    pallas_call x0 -> x2, Pallas kernels: none -> 90.7 us  [the longest x1 48.2 us: local(): pl.pallas_call(functools.partial(pkg_kernel, nd, ng, cap, blocks), out_sh...]
    ppermute x24 -> x0, starting transfers between devices: 66.8 us -> none  [the longest x12 48.6 us: with_halo(): lax.ppermute(tail, axis, [(i, (i + 1) % count) for i in range(ends)])]
    all_to_all x4 -> x0, starting transfers between devices: 35.6 us -> none  [the longest x1 12.6 us: local(): lax.all_to_all(current, 'die', split_axis=0, concat_axis=0, tiled=True)]
    ppermute x24 -> x0, waiting for transfers between devices: 20.8 us -> none  [the longest x12 16.9 us: with_halo(): lax.ppermute(head, axis, [((i + 1) % count, i) for i in range(ends)])]
    all_to_all x4 -> x0, waiting for transfers between devices: 16.7 us -> none  [the longest x1 7.33 us: local(): lax.all_to_all(current, 'die', split_axis=0, concat_axis=0, tiled=True)]
  transfers between devices with their start and end apart: 29 -> 0, of which waited for: 13 -> 0; matrix products, arithmetic and copies ran while one was open for 25% -> 0% of each run, Pallas kernels for 0% -> 0%
where the time goes in v1:
time: 96.2 us; the launch traced here: 96 us
  Pallas kernels  90.7 us (94%)
  local copies, waits for them, and re-layouts  4.6 us (5%)
    pallas_call x1, Pallas kernels, local(): pl.pallas_call(functools.partial(pkg_kernel, nd, ng, cap, blocks), out_sh...  48.2 us
    pallas_call x1, Pallas kernels, local(): pl.pallas_call(functools.partial(die_kernel, nd, ng, cap, blocks), out_sh...  42.6 us
    unnamed x7, local copies, waits for them, and re-layouts  3.15 us

profile of v1, /device:TPU:1, one launch (start us, length us, event | category | flops | bytes accessed | tf_op | source)
XLA Modules:
  0.0 96.0 jit_solution(3636385219063596725)
XLA Ops:
  0.6 0.7 broadcast_in_dim.7
  1.4 0.7 broadcast_in_dim.8.ids_ref
  2.1 42.6 %die_round.1 = (f32[128,256]{1,0:T(8,128)}, f32[72,128]{1,0:T(8,128)}, s32[64,128]{1,0:T(8,128)}) custom-call(f32[128,256]{1,0:T(8,128)} %volt_ref.1, f32[128,256]{1,0:T(8,128)} %load_ref.1, f32[128,256]{1,0:T(8,128)} %shunt_ref.1, s32[64,128]{1,0:T(8,128)} %node_ref.1, s32[16,4,128]{2,1,0:T(4,128)} %broadcast_in_dim.8.ids_ref, f32[64,128]{1,0:T(8,128)} %cond_ref.1, ...), custom_call_target="tpu_custom_call" | custom-call | tf_op jit(solution)/shard_map/die_round/pallas_call | solution.py:537
  44.6 0.0 copy-start
  44.6 48.2 %package_round.1 = (f32[1024,128]{1,0:T(8,128)}, f32[64,128]{1,0:T(8,128)}) custom-call(f32[72,128]{1,0:T(8,128)} %get-tuple-element.9.item_ref, s32[64,128]{1,0:T(8,128)} %get-tuple-element.10.rids_ref, f32[1024,128]{1,0:T(8,128)} %pkg_ref.3, f32[1024,128]{1,0:T(8,128)} %diag_ref.1, s32[4,1024]{1,0:T(4,128)} %pat_ref.1, f32[4,1024]{1,0:T(4,128)} %wt_ref.1, ...), custom_call_target="tpu_custom_call" | custom-call | tf_op jit(solution)/shard_map/package_round/pallas_call | solution.py:561
  92.8 0.0 copy-done
  92.9 0.7 copy.17
  93.5 0.0 copy-start.1
  93.5 1.9 %copy.18 = f32[1024,128]{1,0:T(8,128)} copy(f32[1024,128]{1,0:T(8,128)} %get-tuple-element.17) | data formatting | bytes 1048576
  95.4 0.0 copy-done.1
  95.4 0.6 copy.19
Async XLA Ops:
  44.6 48.2 %copy-start = (f32[128,256]{1,0:T(8,128)S(1)}, f32[128,256]{1,0:T(8,128)}, u32[]{:S(2)}) copy-start(f32[128,256]{1,0:T(8,128)} %get-tuple-element.16) | copy-start | bytes 393220
  93.5 1.9 %copy-start.1 = (f32[64,128]{1,0:T(8,128)S(1)}, f32[64,128]{1,0:T(8,128)}, u32[]{:S(2)}) copy-start(f32[64,128]{1,0:T(8,128)} %get-tuple-element.18) | copy-start | bytes 98308

commit v2 on v0

v2 whole, which is shorter than its diff:
```python
import functools
import math

import jax
import jax.numpy as jnp
from jax import lax
from jax.experimental import pallas as pl
from jax.experimental.pallas import tpu as pltpu
from jax.sharding import PartitionSpec as P

SWEEPS = 4
ITERS = 4
MESH = pl.DeviceIdType.MESH
F32 = jnp.float32
BF16 = jnp.bfloat16


def sweep_weights(sweeps):
    return [
        1.0 / (1.0 + 0.8 * math.cos(math.pi * (2 * index + 1) / (2 * sweeps)))
        for index in range(sweeps)
    ]


def split(x):
    hi = x.astype(BF16)
    lo = (x - hi.astype(F32)).astype(BF16)
    return hi, lo


def remote(src, dst, send_sem, recv_sem, **device):
    return pltpu.make_async_remote_copy(
        src_ref=src,
        dst_ref=dst,
        send_sem=send_sem,
        recv_sem=recv_sem,
        device_id=device,
        device_id_type=MESH,
    )


class Exchange:
    def __init__(self, count, me, src, dst, sems, grp=None):
        self.me = me
        self.src, self.dst = src, dst
        self.copies = []
        for k in range(1 if grp is None else 0, count):
            to = lax.rem(me + k, count)
            where = {"die": to} if grp is None else {"grp": grp, "die": to}
            self.copies.append(
                remote(src.at[to], dst.at[me], sems.at[0, k], sems.at[1, k], **where)
            )

    def start(self):
        for copy in self.copies:
            copy.start()

    def keep(self):
        self.dst[self.me] = self.src[self.me]

    def wait(self):
        for copy in self.copies:
            copy.wait_recv()

    def drain(self):
        for copy in self.copies:
            copy.wait_send()


def kernel(
    nd, ng, cap, blocks,
    block_ref, node_ref, cond_ref,
    volt_hbm, load_hbm, shunt_hbm, pkg_hbm, diag_hbm, pat_hbm, wt_hbm, coup_hbm,
    die_hbm, plane_hbm, bump_hbm,
    volt_ref, load_ref, shunt_ref, coup_ref, die_v, bump_v,
    ids_out, ids_got, rows_out, rows_got, cur_out, cur_got, cur_part,
    start_ref, hot, planes, onecol, acc, vx, rx, dx,
    edge_n, edge_s, edge_w, edge_e,
    halo_n, halo_s, halo_w, halo_e, halo_nw, halo_ne, halo_sw, halo_se,
    redge_n, redge_s, redge_w, redge_e,
    rhalo_n, rhalo_s, rhalo_w, rhalo_e, rhalo_nw, rhalo_ne, rhalo_sw, rhalo_se,
    items, x_f, x_s, inf_x, pkg_x, diag_x, rdiag, pat_x, wt_x, wmat, total,
    sem_in, sem_outs, sem_ids, sem_rows, sem_cur, sem_cur_part, sem_halo, sem_rhalo,
    sem_const, sem_ids_part, sem_ring, sem_core, sem_inf, sem_bump,
):
    me, mg = lax.axis_index("die"), lax.axis_index("grp")
    rows, cols = volt_ref.shape
    nblk = node_ref.shape[0]
    ext = blocks + 256
    tiles = ext // 128
    ny = ng // 4
    half = ny // 2
    c = lax.rem(mg, 2)
    y = lax.rem(mg // 2, ny)
    h = mg // (2 * ny)

    def index(hh, yy, cc):
        return (hh * ny + yy) * 2 + cc

    up, down = lax.rem(mg + ng - 1, ng), lax.rem(mg + 1, ng)
    west, east = lax.rem(me + nd - 1, nd), lax.rem(me + 1, nd)
    plus, minus = lax.rem(y + 1, ny), lax.rem(y + ny - 1, ny)
    right, left = index(h, plus, c), index(h, minus, c)
    core, part = index(h, y, 1 - c), index(1 - h, y, c)

    own = pl.ds(128, blocks)
    own_lanes = slice(128, 128 + blocks)
    loads = [
        pltpu.make_async_copy(src, dst, sem_in.at[k])
        for k, (src, dst) in enumerate(
            (
                (pkg_hbm, pkg_x.at[own]),
                (diag_hbm, diag_x.at[own]),
                (pat_hbm, pat_x.at[:, own_lanes]),
                (wt_hbm, wt_x.at[:, own_lanes]),
                (shunt_hbm, shunt_ref),
                (volt_hbm, volt_ref),
                (load_hbm, load_ref),
                (coup_hbm, coup_ref),
            )
        )
    ]
    for copy in loads:
        copy.start()

    barrier = pltpu.get_barrier_semaphore()

    def signal(**device):
        pl.semaphore_signal(barrier, inc=1, device_id=device, device_id_type=MESH)

    for k in range(1, nd):
        signal(die=lax.rem(me + k, nd))
    for g in (up, down):
        for d in (west, me, east):
            signal(grp=g, die=d)
    for g in (right, left, core):
        signal(grp=g)
    for k in range(nd):
        signal(grp=part, die=lax.rem(me + k, nd))

    for s in range(nblk):
        ids_out[s // cap, s % cap : s % cap + 1, :] = jnp.full((1, 128), block_ref[s], jnp.int32)

    chunk = 8
    steps = nblk // chunk
    shift = cols.bit_length() - 1

    def one_columns(it, carry):
        node = node_ref[pl.ds(pl.multiple_of(it * chunk, chunk), chunk), :]
        col = jnp.bitwise_and(node, cols - 1)
        for i in range(chunk):
            iota = lax.broadcasted_iota(jnp.int32, (cols, 128), 0)
            onecol[it * chunk + i] = jnp.where(iota == col[i : i + 1, :], 1.0, 0.0).astype(BF16)
        return carry

    lax.fori_loop(0, steps, one_columns, 0)
    pl.semaphore_wait(barrier, (nd - 1) + 6 + 3 + nd)

    ids = Exchange(nd, me, ids_out, ids_got, sem_ids)
    ids.start()
    ids.keep()

    for copy in loads[:4]:
        copy.wait()
    tail, head = pl.ds(128 + blocks, 128), pl.ds(0, 128)
    first, last = pl.ds(128, 128), pl.ds(blocks, 128)
    lt, ll = slice(128 + blocks, 256 + blocks), slice(blocks, 128 + blocks)
    lh, lf = slice(0, 128), slice(128, 256)
    consts = [
        remote(src, dst, sem_const.at[0, k], sem_const.at[1, k], die=west if k < 4 else east)
        for k, (src, dst) in enumerate(
            (
                (pkg_x.at[first], pkg_x.at[tail]),
                (diag_x.at[first], diag_x.at[tail]),
                (pat_x.at[:, lf], pat_x.at[:, lt]),
                (wt_x.at[:, lf], wt_x.at[:, lt]),
                (pkg_x.at[last], pkg_x.at[head]),
                (diag_x.at[last], diag_x.at[head]),
                (pat_x.at[:, ll], pat_x.at[:, lh]),
                (wt_x.at[:, ll], wt_x.at[:, lh]),
            )
        )
    ]
    for copy in consts:
        copy.start()

    row_iota = lax.broadcasted_iota(jnp.int32, (rows, 128), 0)

    def scatter(value_of, slot):
        def step(it, carry):
            at = pl.ds(pl.multiple_of(it * chunk, chunk), chunk)
            node = node_ref[at, :]
            row = jnp.right_shift(node, shift)
            hi, lo = [v.astype(F32) for v in split(value_of(at))]
            parts_hi, parts_lo = [], []
            for i in range(chunk):
                here = row_iota == row[i : i + 1, :]
                parts_hi.append(jnp.where(here, hi[i : i + 1, :], 0.0).astype(BF16))
                parts_lo.append(jnp.where(here, lo[i : i + 1, :], 0.0).astype(BF16))
            lhs = jnp.concatenate(
                [jnp.concatenate(parts_hi, axis=1), jnp.concatenate(parts_lo, axis=1)], axis=0
            )
            rhs = jnp.concatenate([onecol[it * chunk + i] for i in range(chunk)], axis=1)
            both = lax.dot_general(
                lhs, rhs, (((1,), (1,)), ((), ())), preferred_element_type=F32
            )
            acc[slot] += both[:rows] + both[rows:]
            return carry

        acc[slot] = jnp.zeros((rows, cols), F32)
        lax.fori_loop(0, steps, step, 0)

    loads[4].wait()
    scatter(lambda at: jnp.where(node_ref[at, :] >= 0, cond_ref[at, :], 0.0), 0)

    def halo_copies(en, es, ew, ee, n, s, w, e, nw, ne, sw, se, sems):
        return [
            remote(src, dst, sems.at[0, k], sems.at[1, k], grp=g, die=d)
            for k, (src, dst, g, d) in enumerate(
                (
                    (en, s, up, me),
                    (es, n, down, me),
                    (ew, e, mg, west),
                    (ee, w, mg, east),
                    (en.at[0], se, up, west),
                    (en.at[1], sw, up, east),
                    (es.at[0], ne, down, west),
                    (es.at[1], nw, down, east),
                )
            )
        ]

    middle = (slice(8, 8 + rows), slice(128, 128 + cols))

    def set_edges(k, ext_ref, tile, en, es, ew, ee):
        at = slice(8 * k, 8 * k + 8)
        ext_ref[middle] = tile
        for b in range(2):
            side = slice(b * (cols - 128), b * (cols - 128) + 128)
            en[b, at, :] = tile[:8, side]
            es[b, at, :] = tile[rows - 8 :, side]
        ew[at, :] = jnp.transpose(tile[:, :128])[:8]
        ee[at, :] = jnp.transpose(tile[:, cols - 128 :])[120:]

    pad = jnp.zeros((120, 128), F32)

    def set_halos(k, ext_ref, n, s, w, e, nw, ne, sw, se):
        at = slice(8 * k, 8 * k + 8)
        for b in range(2):
            side = slice(128 + b * (cols - 128), 256 + b * (cols - 128))
            ext_ref[0:8, side] = n[b, at, :]
            ext_ref[8 + rows :, side] = s[b, at, :]
        ext_ref[8 : 8 + rows, 0:128] = jnp.transpose(jnp.concatenate([pad, w[at, :]], axis=0))
        ext_ref[8 : 8 + rows, 128 + cols :] = jnp.transpose(
            jnp.concatenate([e[at, :], pad], axis=0)
        )
        ext_ref[0:8, 0:128] = nw[at, :]
        ext_ref[0:8, 128 + cols :] = ne[at, :]
        ext_ref[8 + rows :, 0:128] = sw[at, :]
        ext_ref[8 + rows :, 128 + cols :] = se[at, :]

    edges = (edge_n, edge_s, edge_w, edge_e)
    halos = (halo_n, halo_s, halo_w, halo_e, halo_nw, halo_ne, halo_sw, halo_se)
    redges = (redge_n, redge_s, redge_w, redge_e)
    rhalos = (rhalo_n, rhalo_s, rhalo_w, rhalo_e, rhalo_nw, rhalo_ne, rhalo_sw, rhalo_se)

    planes[...] = jnp.concatenate(split(pkg_x[own, :]), axis=1)
    ids.wait()
    wanted = jnp.concatenate([ids_got[j] for j in range(nd)], axis=0)
    near = wanted - (lax.broadcasted_iota(jnp.int32, wanted.shape, 1) + me * blocks)
    for q in range(blocks // 256):
        for p in range(2):
            hot[q, :, 128 * p : 128 * p + 128] = jnp.where(
                near == 256 * q + 128 * p, 1.0, 0.0
            ).astype(BF16)

    def pick_rows(source, offset, into):
        into[...] = jnp.zeros_like(into)

        def step(q, carry):
            at = pl.ds(pl.multiple_of(offset + q * 256, 64), 256)
            both = jnp.dot(hot[q], source[at, :], preferred_element_type=F32)
            into[...] += both[:, :128] + both[:, 128:]
            return carry

        lax.fori_loop(0, blocks // 256, step, 0)

    pick_rows(planes, 0, start_ref)
    for j in range(nd):
        rows_out[j] = start_ref[j * cap : (j + 1) * cap, :]
    rows_x = Exchange(nd, me, rows_out, rows_got, sem_rows)
    rows_x.start()
    rows_x.keep()

    lane = lax.broadcasted_iota(jnp.int32, (nblk, 128), 1)
    sub = lax.broadcasted_iota(jnp.int32, (nblk, 128), 0)
    mine = jnp.logical_or(lane == sub, lane == sub + 64)
    in_lanes = jnp.sum(jnp.where(mine, wanted.astype(F32), 0.0), axis=0, keepdims=True)
    id_rows = pl.ds(nblk, 8)
    items[mg, nblk:, :] = jnp.broadcast_to(in_lanes, (8, 128))
    ids_part = remote(
        items.at[mg, id_rows], items.at[mg, id_rows], sem_ids_part.at[0], sem_ids_part.at[1],
        grp=part,
    )
    ids_part.start()

    loads[5].wait()
    inverse = 1.0 / (4.0 + shunt_ref[...] + acc[0])
    set_edges(0, vx, volt_ref[...], *edges)
    set_edges(1, dx, inverse, *edges)
    early = halo_copies(*edges, *halos, sem_halo)
    for copy in early:
        copy.start()

    def build(t, carry):
        at = pl.ds(pl.multiple_of(t * 128, 128), 128)
        ids_at = pat_x[:, at] + (128 + 64 - me * blocks - t * 128)
        weights = wt_x[:, at]
        source = lax.broadcasted_iota(jnp.int32, (256, 128), 0)
        matrix = jnp.zeros((256, 128), F32)
        for k in range(ids_at.shape[0]):
            matrix += jnp.where(source == ids_at[k : k + 1, :], weights[k : k + 1, :], 0.0)
        wmat[t] = jnp.concatenate(split(jnp.transpose(matrix)), axis=0)
        return carry

    lax.fori_loop(1, tiles - 1, build, 0)

    rows_x.wait()
    for j in range(nd):
        start_ref[j * cap : (j + 1) * cap, :] = rows_got[j]
    scatter(
        lambda at: jnp.where(node_ref[at, :] >= 0, cond_ref[at, :] * start_ref[at, :], 0.0), 1
    )
    loads[6].wait()
    set_edges(0, rx, acc[1] - load_ref[...], *redges)
    late = halo_copies(*redges, *rhalos, sem_rhalo)
    for copy in late:
        copy.start()
    for copy in early:
        copy.wait_recv()
    set_halos(0, vx, *halos)
    set_halos(1, dx, *halos)
    height, width = rows + 16, cols + 256
    grow = lax.broadcasted_iota(jnp.int32, (height, width), 0) + (mg * rows - 8)
    gcol = lax.broadcasted_iota(jnp.int32, (height, width), 1) + (me * cols - 128)
    inside = (grow >= 0) & (grow < ng * rows) & (gcol >= 0) & (gcol < nd * cols)
    v = jnp.where(inside, vx[...], 0.0)
    for copy in late:
        copy.wait_recv()
    set_halos(0, rx, *rhalos)
    r = rx[...]
    inv = dx[...]
    for weight in sweep_weights(SWEEPS):
        beside = (
            pltpu.roll(v, 1, 0)
            + pltpu.roll(v, height - 1, 0)
            + pltpu.roll(v, 1, 1)
            + pltpu.roll(v, width - 1, 1)
        )
        v = jnp.where(inside, v + weight * ((r + beside) * inv - v), 0.0)
    final = v[middle]
    die_v[...] = final
    die_done = pltpu.make_async_copy(die_v, die_hbm, sem_outs.at[0])
    die_done.start()
    halves = jnp.concatenate(split(final), axis=0)

    def currents(it, carry):
        at = pl.ds(pl.multiple_of(it * chunk, chunk), chunk)
        node = node_ref[at, :]
        row = jnp.right_shift(node, shift)
        rhs = jnp.concatenate([onecol[it * chunk + i] for i in range(chunk)], axis=1)
        both = jnp.dot(halves, rhs, preferred_element_type=F32)
        by_row = both[:rows] + both[rows:]
        seen = [
            jnp.sum(
                jnp.where(row_iota == row[i : i + 1, :], by_row[:, 128 * i : 128 * i + 128], 0.0),
                axis=0,
                keepdims=True,
            )
            for i in range(chunk)
        ]
        flow = jnp.where(
            node >= 0, cond_ref[at, :] * (start_ref[at, :] - jnp.concatenate(seen, axis=0)), 0.0
        )
        for i in range(chunk // cap):
            cur_out[it * (chunk // cap) + i] = flow[i * cap : (i + 1) * cap]
        return carry

    lax.fori_loop(0, steps, currents, 0)
    cur_x = Exchange(nd, me, cur_out, cur_got, sem_cur)
    cur_p = Exchange(nd, me, cur_out, cur_part, sem_cur_part, grp=part)
    cur_x.start()
    cur_p.start()
    cur_x.keep()

    for copy in consts:
        copy.wait_recv()
    lax.fori_loop(0, 2, lambda i, carry: build(i * (tiles - 1), carry), 0)
    rdiag[...] = 1.0 / diag_x[...]
    for q in range(ITERS + 1):
        x_s[q, 0:64, :] = jnp.zeros((64, 256), BF16)
        x_s[q, 64 + ext :, :] = jnp.zeros((64, 256), BF16)
    x_s[0, 64 : 64 + ext, :] = jnp.concatenate(split(pkg_x[...]), axis=1)
    inf_x[0:32, :] = jnp.zeros((32, 128), F32)
    inf_x[ext - 32 :, :] = jnp.zeros((32, 128), F32)
    total[...] = jnp.zeros((blocks, 256), F32)
    loads[7].wait()

    sent = []
    core_of = {}

    def pass_on(slot, direction, dist, k):
        copy = remote(
            items.at[slot], items.at[slot],
            sem_ring.at[0, direction, dist, k], sem_ring.at[1, direction, dist, k],
            grp=right if direction == 0 else left,
        )
        copy.start()
        sent.append(copy)

    def to_core(slot, key):
        n = len(core_of)
        copy = remote(
            items.at[slot], items.at[slot], sem_core.at[0, n], sem_core.at[1, n], grp=core
        )
        copy.start()
        core_of[key] = copy

    def held(direction, dist, k, cc):
        yy = lax.rem(y + ny - dist, ny) if direction == 0 else lax.rem(y + dist, ny)
        return index(h if k == 0 else 1 - h, yy, cc)

    reach = {(0, 0): half, (0, 1): half - 1, (1, 0): half - 1, (1, 1): half}
    first_lanes = lax.broadcasted_iota(jnp.int32, (1, 128), 1) < 64

    def add_group(slots):
        def ids_of(slot):
            return items[slot, nblk : nblk + 1, :]

        pair_ids = [
            jnp.where(first_lanes, ids_of(slots[2 * p]), ids_of(slots[2 * p + 1])).astype(
                jnp.int32
            )
            - me * blocks
            for p in range(2)
        ]
        flows = []
        for slot in slots:
            flows.append(items[slot, :nblk, :])
            if nblk < 64:
                flows.append(jnp.zeros((64 - nblk, 128), F32))
        rhs = jnp.concatenate(split(jnp.concatenate(flows, axis=0)), axis=1)
        planes[0:256, :] = rhs

        def step(q, carry):
            at = pl.ds(pl.multiple_of(q * 256, 256), 256)
            target = lax.broadcasted_iota(jnp.int32, (256, 128), 0) + q * 256
            lhs = jnp.concatenate(
                [jnp.where(target == i, 1.0, 0.0).astype(BF16) for i in pair_ids], axis=1
            )
            total[at, :] += jnp.dot(lhs, planes[0:256, :], preferred_element_type=F32)
            return carry

        lax.fori_loop(0, blocks // 256, step, 0)

    def keys_of(dist):
        keys = [
            (direction, dist, k)
            for k in range(2)
            for direction in range(2)
            if reach[direction, k] >= dist
        ]
        return keys + (["own", "part"] if dist == half else [])

    def group(dist, cc):
        slots = []
        for key in keys_of(dist):
            if key == "own":
                slots.append(index(h, y, cc))
            elif key == "part":
                slots.append(index(1 - h, y, cc))
            else:
                slots.append(held(*key, cc))
        return slots

    def core_group(dist):
        for key in keys_of(dist):
            core_of[key].wait_recv()
        add_group(group(dist, 1 - c))

    cur_x.wait()
    for j in range(nd):
        items[mg, j * cap : (j + 1) * cap, :] = cur_got[j]
    for direction in range(2):
        if reach[direction, 0] >= 1:
            pass_on(mg, direction, 1, 0)
    to_core(mg, "own")
    ids_part.wait_recv()
    cur_p.wait()
    for j in range(nd):
        items[part, j * cap : (j + 1) * cap, :] = cur_part[j]
    for direction in range(2):
        if reach[direction, 1] >= 1:
            pass_on(part, direction, 1, 1)
    to_core(part, "part")
    for dist in range(1, half + 1):
        for k in range(2):
            for direction in range(2):
                if reach[direction, k] >= dist:
                    slot = held(direction, dist, k, c)
                    remote(
                        items.at[slot], items.at[slot],
                        sem_ring.at[0, direction, dist, k], sem_ring.at[1, direction, dist, k],
                        grp=right if direction == 0 else left,
                    ).wait_recv()
                    if reach[direction, k] >= dist + 1:
                        pass_on(slot, direction, dist + 1, k)
                    to_core(slot, (direction, dist, k))
        add_group(group(dist, c))
        if dist > 1:
            core_group(dist - 1)
    core_group(half)

    inf_x[own, :] = total[:, :128] + total[:, 128:]
    infs = [
        remote(
            inf_x.at[pl.ds(src, 96)], inf_x.at[pl.ds(dst, 96)],
            sem_inf.at[0, k], sem_inf.at[1, k], die=to,
        )
        for k, (src, dst, to) in enumerate(
            ((128, 128 + blocks, west), (32 + blocks, 32, east))
        )
    ]
    for copy in infs:
        copy.start()
    coup = jnp.concatenate(split(coup_ref[...]), axis=1)

    def tile(iteration, t):
        start = pl.multiple_of(t * 128, 128)
        at = pl.ds(start, 128)
        near = jnp.dot(
            wmat[t], x_s[iteration - 1, pl.ds(start, 256), :], preferred_element_type=F32
        )
        here = x_s[iteration - 1, pl.ds(start + 64, 128), :]
        both = jnp.concatenate([here[:, :128], here[:, 128:]], axis=0)
        coupled = near + jnp.dot(both, coup, preferred_element_type=F32)
        coupled = coupled[:128] + coupled[128:]
        coupled = coupled[:, :128] + coupled[:, 128:]
        value = (-inf_x[at, :] - coupled) * rdiag[at, :]
        if iteration == ITERS:
            x_f[at, :] = value
        x_s[iteration, pl.ds(start + 64, 128), :] = jnp.concatenate(split(value), axis=1)

    def pairs(iteration, begin, end):
        def step(i, carry):
            tile(iteration, i)
            tile(iteration, tiles - 1 - i)
            return carry

        if end > begin:
            lax.fori_loop(begin, end, step, 0)

    deep = tiles // 2
    for iteration in range(1, ITERS + 1):
        pairs(iteration, min(iteration, deep), deep)
    for copy in infs:
        copy.wait_recv()
    for iteration in range(1, ITERS + 1):
        pairs(iteration, 1 if iteration == ITERS else 0, min(iteration, deep))

    plane_done = pltpu.make_async_copy(x_f.at[own], plane_hbm, sem_outs.at[1])
    plane_done.start()
    rows_x.drain()
    pick_rows(x_s.at[ITERS], 64 + 128, start_ref)
    for j in range(nd):
        rows_out[j] = start_ref[j * cap : (j + 1) * cap, :]
    bump_x = Exchange(nd, me, rows_out, rows_got, sem_bump)
    bump_x.start()
    bump_x.keep()
    for x in (ids, cur_x, cur_p):
        x.drain()
    for copy in sent + list(core_of.values()) + [ids_part] + consts + infs + early + late:
        copy.wait_send()
    bump_x.wait()
    for j in range(nd):
        bump_v[j * cap : (j + 1) * cap, :] = rows_got[j]
    bump_done = pltpu.make_async_copy(bump_v, bump_hbm, sem_outs.at[2])
    bump_done.start()
    bump_x.drain()
    die_done.wait()
    plane_done.wait()
    bump_done.wait()


def local(
    nd, ng,
    die_volt, die_load, die_shunt, bump_node, bump_block, bump_cond,
    pkg_volt, pkg_diag, pkg_pattern, pkg_weight, block_coupling,
):
    nblk = bump_node.shape[0]
    cap = nblk // nd
    blocks = pkg_volt.shape[0]
    rows, cols = die_volt.shape
    ext = blocks + 256
    knb = pkg_pattern.shape[0]
    vmem = pl.BlockSpec(memory_space=pltpu.VMEM)
    anywhere = pl.BlockSpec(memory_space=pl.ANY)
    dma = pltpu.SemaphoreType.DMA

    def buf(*shape, dtype=F32):
        return pltpu.VMEM(shape, dtype)

    def strip_set(depth):
        return [
            buf(2, depth, 128), buf(2, depth, 128), buf(depth, 128), buf(depth, 128),
            buf(2, depth, 128), buf(2, depth, 128), buf(depth, 128), buf(depth, 128),
            buf(depth, 128), buf(depth, 128), buf(depth, 128), buf(depth, 128),
        ]

    return pl.pallas_call(
        functools.partial(kernel, nd, ng, cap, blocks),
        out_shape=(
            jax.ShapeDtypeStruct((rows, cols), F32),
            jax.ShapeDtypeStruct((blocks, 128), F32),
            jax.ShapeDtypeStruct((nblk, 128), F32),
        ),
        in_specs=[pl.BlockSpec(memory_space=pltpu.SMEM), vmem, vmem] + [anywhere] * 8,
        out_specs=(anywhere,) * 3,
        scratch_shapes=[
            buf(rows, cols), buf(rows, cols), buf(rows, cols), buf(128, 128),
            buf(rows, cols), buf(nblk, 128),
            buf(nd, cap, 128, dtype=jnp.int32), buf(nd, cap, 128, dtype=jnp.int32),
            buf(nd, cap, 128), buf(nd, cap, 128),
            buf(nd, cap, 128), buf(nd, cap, 128), buf(nd, cap, 128),
            buf(nblk, 128),
            buf(blocks // 256, nblk, 256, dtype=BF16),
            buf(blocks, 256, dtype=BF16),
            buf(nblk, cols, 128, dtype=BF16),
            buf(2, rows, cols),
            buf(rows + 16, cols + 256), buf(rows + 16, cols + 256), buf(rows + 16, cols + 256),
            *strip_set(16),
            *strip_set(8),
            buf(ng, nblk + 8, 128),
            buf(ext, 128),
            buf(ITERS + 1, ext + 128, 256, dtype=BF16),
            buf(ext, 128),
            buf(ext, 128), buf(ext, 128), buf(ext, 128),
            buf(knb, ext, dtype=jnp.int32), buf(knb, ext),
            buf(ext // 128, 256, 256, dtype=BF16),
            buf(blocks, 256),
            dma((8,)), dma((3,)), dma((2, nd)), dma((2, nd)), dma((2, nd)), dma((2, nd)),
            dma((2, 8)), dma((2, 8)), dma((2, 8)), dma((2,)),
            dma((2, 2, ng // 8 + 2, 2)), dma((2, ng // 2)), dma((2, 2)), dma((2, nd)),
        ],
        compiler_params=pltpu.CompilerParams(collective_id=0, has_side_effects=True),
        name="coupling_round",
    )(
        bump_block, bump_node, bump_cond, die_volt, die_load, die_shunt,
        pkg_volt, pkg_diag, pkg_pattern, pkg_weight, block_coupling,
    )


def solution(mesh):
    return jax.shard_map(
        functools.partial(local, mesh.shape["die"], mesh.shape["grp"]),
        mesh=mesh,
        in_specs=(
            P("grp", "die"),
            P("grp", "die"),
            P("grp", "die"),
            P(("grp", "die"), None),
            P(("grp", "die")),
            P(("grp", "die"), None),
            P("die", None),
            P("die", None),
            P(None, "die"),
            P(None, "die"),
            P(),
        ),
        out_specs=(P("grp", "die"), P("die", None), P(("grp", "die"), None)),
        check_vma=False,
    )
```

time: 655 us -> 81 us (0.12)
  waiting for transfers between devices: 305 us -> 0 us
  other arithmetic: 106 us -> 0 us
  local copies, waits for them, and re-layouts: 108 us -> 4.06 us
  starting transfers between devices: 102 us -> 0 us
  Pallas kernels: 0 us -> 75.8 us
  between operations: 14.9 us -> 0.64 us
  blocking collectives: 12.1 us -> 0 us
    psum x1 -> x0, waiting for transfers between devices: 267 us -> none  [local(): inflow = lax.psum(local_sum, 'grp')]
    gather x19 -> x0, local copies, waits for them, and re-layouts: 102 us -> none  [the longest x16 53.5 us: local(): extended[local_index[neighbour]]]
    scatter-add x3 -> x0, other arithmetic: 95.4 us -> none  [the longest x1 46.9 us: local(): flat_zero.at[safe_node].add(conductance.reshape(-1))]
    pallas_call x0 -> x1, Pallas kernels: none -> 75.8 us  [local(): pl.pallas_call(functools.partial(kernel, nd, ng, cap, blocks), out_shape=...]
    ppermute x24 -> x0, starting transfers between devices: 66.8 us -> none  [the longest x12 48.6 us: with_halo(): lax.ppermute(tail, axis, [(i, (i + 1) % count) for i in range(ends)])]
    all_to_all x4 -> x0, starting transfers between devices: 35.6 us -> none  [the longest x1 12.6 us: local(): lax.all_to_all(current, 'die', split_axis=0, concat_axis=0, tiled=True)]
    ppermute x24 -> x0, waiting for transfers between devices: 20.8 us -> none  [the longest x12 16.9 us: with_halo(): lax.ppermute(head, axis, [((i + 1) % count, i) for i in range(ends)])]
    all_to_all x4 -> x0, waiting for transfers between devices: 16.7 us -> none  [the longest x1 7.33 us: local(): lax.all_to_all(current, 'die', split_axis=0, concat_axis=0, tiled=True)]
  transfers between devices with their start and end apart: 29 -> 0, of which waited for: 13 -> 0; matrix products, arithmetic and copies ran while one was open for 25% -> 0% of each run, Pallas kernels for 0% -> 0%
where the time goes in v2:
time: 81 us; the launch traced here: 80.5 us
  Pallas kernels  75.8 us (94%)
  local copies, waits for them, and re-layouts  4.06 us (5%)
    pallas_call x1, Pallas kernels, local(): pl.pallas_call(functools.partial(kernel, nd, ng, cap, blocks), out_shape=...  75.8 us
    unnamed x5, local copies, waits for them, and re-layouts  4.06 us

profile of v2, /device:TPU:1, one launch (start us, length us, event | category | flops | bytes accessed | tf_op | source)
XLA Modules:
  0.0 80.5 jit_solution(1297646346299743387)
XLA Ops:
  0.6 75.8 %coupling_round.1 = (f32[128,256]{1,0:T(8,128)}, f32[1024,128]{1,0:T(8,128)}, f32[64,128]{1,0:T(8,128)}) custom-call(s32[64]{0:T(128)} %block_ref.1, s32[64,128]{1,0:T(8,128)} %node_ref.1, f32[64,128]{1,0:T(8,128)} %cond_ref.1, f32[128,256]{1,0:T(8,128)} %volt_hbm.1, f32[128,256]{1,0:T(8,128)} %load_hbm.1, f32[128,256]{1,0:T(8,128)} %shunt_hbm.1, ...), custom_call_target="tpu_custom_call" | custom-call | tf_op jit(solution)/shard_map/coupling_round/pallas_call | solution.py:620
  76.5 1.6 %copy.17 = f32[128,256]{1,0:T(8,128)} copy(f32[128,256]{1,0:T(8,128)} %get-tuple-element.6) | data formatting | bytes 262144
  78.1 0.0 copy-start
  78.1 1.9 %copy.18 = f32[1024,128]{1,0:T(8,128)} copy(f32[1024,128]{1,0:T(8,128)} %get-tuple-element.7) | data formatting | bytes 1048576
  79.9 0.0 copy-done
  79.9 0.6 copy.19
Async XLA Ops:
  78.1 1.9 %copy-start = (f32[64,128]{1,0:T(8,128)S(1)}, f32[64,128]{1,0:T(8,128)}, u32[]{:S(2)}) copy-start(f32[64,128]{1,0:T(8,128)} %get-tuple-element.8) | copy-start | bytes 98308

commit v3 on v2

--- a/solution.py
+++ b/solution.py
@@ -208,7 +208,12 @@
             return carry
 
         acc[slot] = jnp.zeros((rows, cols), F32)
-        lax.fori_loop(0, steps, step, 0)
+
+        def double(it, carry):
+            step(2 * it, carry)
+            return step(2 * it + 1, carry)
+
+        lax.fori_loop(0, steps // 2, double, 0)
 
     loads[4].wait()
     scatter(lambda at: jnp.where(node_ref[at, :] >= 0, cond_ref[at, :], 0.0), 0)
@@ -275,15 +280,13 @@
             ).astype(BF16)
 
     def pick_rows(source, offset, into):
-        into[...] = jnp.zeros_like(into)
-
-        def step(q, carry):
-            at = pl.ds(pl.multiple_of(offset + q * 256, 64), 256)
-            both = jnp.dot(hot[q], source[at, :], preferred_element_type=F32)
-            into[...] += both[:, :128] + both[:, 128:]
-            return carry
-
-        lax.fori_loop(0, blocks // 256, step, 0)
+        both = jnp.zeros((nblk, 256), F32)
+        for q in range(blocks // 256):
+            both += jnp.dot(
+                hot[q], source[offset + q * 256 : offset + q * 256 + 256, :],
+                preferred_element_type=F32,
+            )
+        into[...] = both[:, :128] + both[:, 128:]
 
     pick_rows(planes, 0, start_ref)
     for j in range(nd):
@@ -386,7 +389,12 @@
             cur_out[it * (chunk // cap) + i] = flow[i * cap : (i + 1) * cap]
         return carry
 
-    lax.fori_loop(0, steps, currents, 0)
+
+    def two_currents(it, carry):
+        currents(2 * it, carry)
+        return currents(2 * it + 1, carry)
+
+    lax.fori_loop(0, steps // 2, two_currents, 0)
     cur_x = Exchange(nd, me, cur_out, cur_got, sem_cur)
     cur_p = Exchange(nd, me, cur_out, cur_part, sem_cur_part, grp=part)
     cur_x.start()
@@ -452,16 +460,18 @@
         rhs = jnp.concatenate(split(jnp.concatenate(flows, axis=0)), axis=1)
         planes[0:256, :] = rhs
 
+        depth = min(blocks, 512)
+
         def step(q, carry):
-            at = pl.ds(pl.multiple_of(q * 256, 256), 256)
-            target = lax.broadcasted_iota(jnp.int32, (256, 128), 0) + q * 256
+            at = pl.ds(pl.multiple_of(q * depth, depth), depth)
+            target = lax.broadcasted_iota(jnp.int32, (depth, 128), 0) + q * depth
             lhs = jnp.concatenate(
                 [jnp.where(target == i, 1.0, 0.0).astype(BF16) for i in pair_ids], axis=1
             )
             total[at, :] += jnp.dot(lhs, planes[0:256, :], preferred_element_type=F32)
             return carry
 
-        lax.fori_loop(0, blocks // 256, step, 0)
+        lax.fori_loop(0, blocks // depth, step, 0)
 
     def keys_of(dist):
         keys = [
@@ -536,7 +546,7 @@
     coup = jnp.concatenate(split(coup_ref[...]), axis=1)
 
     def tile(iteration, t):
-        start = pl.multiple_of(t * 128, 128)
+        start = t * 128
         at = pl.ds(start, 128)
         near = jnp.dot(
             wmat[t], x_s[iteration - 1, pl.ds(start, 256), :], preferred_element_type=F32
@@ -552,13 +562,9 @@
         x_s[iteration, pl.ds(start + 64, 128), :] = jnp.concatenate(split(value), axis=1)
 
     def pairs(iteration, begin, end):
-        def step(i, carry):
+        for i in range(begin, end):
             tile(iteration, i)
             tile(iteration, tiles - 1 - i)
-            return carry
-
-        if end > begin:
-            lax.fori_loop(begin, end, step, 0)
 
     deep = tiles // 2
     for iteration in range(1, ITERS + 1):
@@ -617,7 +623,7 @@
             buf(depth, 128), buf(depth, 128), buf(depth, 128), buf(depth, 128),
         ]
 
-    return pl.pallas_call(
+    results = pl.pallas_call(
         functools.partial(kernel, nd, ng, cap, blocks),
         out_shape=(
             jax.ShapeDtypeStruct((rows, cols), F32),
@@ -658,6 +664,38 @@
         bump_block, bump_node, bump_cond, die_volt, die_load, die_shunt,
         pkg_volt, pkg_diag, pkg_pattern, pkg_weight, block_coupling,
     )
+    return pl.pallas_call(
+        hand_over,
+        out_shape=tuple(jax.ShapeDtypeStruct(r.shape, F32) for r in results),
+        in_specs=[anywhere] * 3,
+        out_specs=(anywhere,) * 3,
+        scratch_shapes=[buf(*r.shape) for r in results] + [dma((2, 16))],
+        name="hand_over",
+    )(*results)
+
+
+def hand_over(*refs):
+    sources, targets, held, sem = refs[:3], refs[3:6], refs[6:9], refs[9]
+    pieces = []
+    for k, (src, dst, mid) in enumerate(zip(sources, targets, held)):
+        count = 8 if k == 1 else 2
+        depth = src.shape[0] // count
+        for p in range(count):
+            at = pl.ds(p * depth, depth)
+            pieces.append((src.at[at], mid.at[at], dst.at[at]))
+    takes = [
+        pltpu.make_async_copy(src, mid, sem.at[0, n]) for n, (src, mid, _) in enumerate(pieces)
+    ]
+    gives = [
+        pltpu.make_async_copy(mid, dst, sem.at[1, n]) for n, (_, mid, dst) in enumerate(pieces)
+    ]
+    for copy in takes:
+        copy.start()
+    for take, give in zip(takes, gives):
+        take.wait()
+        give.start()
+    for copy in gives:
+        copy.wait()
 
 
 def solution(mesh):

time: 81 us -> 72.6 us (0.90)
  Pallas kernels: 75.8 us -> 71.5 us
  local copies, waits for them, and re-layouts: 4.06 us -> 0 us
    pallas_call x1, Pallas kernels: 75.8 us -> 69.5 us  [local(): pl.pallas_call(functools.partial(kernel, nd, ng, cap, blocks), out_shape=...]
    unnamed x5 -> x0, local copies, waits for them, and re-layouts: 4.06 us -> none
    pallas_call x0 -> x1, Pallas kernels: none -> 2.03 us  [local(): pl.pallas_call(hand_over, out_shape=tuple((jax.ShapeDtypeStruct(r.shape,...]
where the time goes in v3:
time: 72.6 us; the launch traced here: 72.1 us
  Pallas kernels  71.5 us (98%)
    pallas_call x1, Pallas kernels, local(): pl.pallas_call(functools.partial(kernel, nd, ng, cap, blocks), out_shape=...  69.5 us
    pallas_call x1, Pallas kernels, local(): pl.pallas_call(hand_over, out_shape=tuple((jax.ShapeDtypeStruct(r.shape,...  2.03 us

profile of v3, /device:TPU:1, one launch (start us, length us, event | category | flops | bytes accessed | tf_op | source)
XLA Modules:
  0.0 72.1 jit_solution(5600184555259343745)
XLA Ops:
  0.6 69.5 %coupling_round.1 = (f32[128,256]{1,0:T(8,128)}, f32[1024,128]{1,0:T(8,128)}, f32[64,128]{1,0:T(8,128)}) custom-call(s32[64]{0:T(128)} %block_ref.1, s32[64,128]{1,0:T(8,128)} %node_ref.1, f32[64,128]{1,0:T(8,128)} %cond_ref.1, f32[128,256]{1,0:T(8,128)} %volt_hbm.1, f32[128,256]{1,0:T(8,128)} %load_hbm.1, f32[128,256]{1,0:T(8,128)} %shunt_hbm.1, ...), custom_call_target="tpu_custom_call" | custom-call | tf_op jit(solution)/shard_map/coupling_round/pallas_call | solution.py:626
  70.1 2.0 %hand_over.1 = (f32[128,256]{1,0:T(8,128)}, f32[1024,128]{1,0:T(8,128)}, f32[64,128]{1,0:T(8,128)}) custom-call(f32[128,256]{1,0:T(8,128)} %get-tuple-element.6.refs_0_, f32[1024,128]{1,0:T(8,128)} %get-tuple-element.7.refs_1_, f32[64,128]{1,0:T(8,128)} %get-tuple-element.8.refs_2_), custom_call_target="tpu_custom_call" | custom-call | tf_op jit(solution)/shard_map/hand_over/pallas_call | solution.py:667

commit v4 on v3

--- a/solution.py
+++ b/solution.py
@@ -69,18 +69,18 @@
 
 def kernel(
     nd, ng, cap, blocks,
-    block_ref, node_ref, cond_ref,
+    block_hbm, node_hbm, cond_hbm,
     volt_hbm, load_hbm, shunt_hbm, pkg_hbm, diag_hbm, pat_hbm, wt_hbm, coup_hbm,
-    die_hbm, plane_hbm, bump_hbm,
-    volt_ref, load_ref, shunt_ref, coup_ref, die_v, bump_v,
+    die_v, plane_v, bump_v,
+    block_ref, node_ref, cond_ref, volt_ref, load_ref, shunt_ref, coup_ref,
     ids_out, ids_got, rows_out, rows_got, cur_out, cur_got, cur_part,
     start_ref, hot, planes, onecol, acc, vx, rx, dx,
     edge_n, edge_s, edge_w, edge_e,
     halo_n, halo_s, halo_w, halo_e, halo_nw, halo_ne, halo_sw, halo_se,
     redge_n, redge_s, redge_w, redge_e,
     rhalo_n, rhalo_s, rhalo_w, rhalo_e, rhalo_nw, rhalo_ne, rhalo_sw, rhalo_se,
-    items, x_f, x_s, inf_x, pkg_x, diag_x, rdiag, pat_x, wt_x, wmat, total,
-    sem_in, sem_outs, sem_ids, sem_rows, sem_cur, sem_cur_part, sem_halo, sem_rhalo,
+    items, x_s, inf_x, pkg_x, diag_x, rdiag, pat_x, wt_x, wmat, total,
+    sem_in, sem_ids, sem_rows, sem_cur, sem_cur_part, sem_halo, sem_rhalo,
     sem_const, sem_ids_part, sem_ring, sem_core, sem_inf, sem_bump,
 ):
     me, mg = lax.axis_index("die"), lax.axis_index("grp")
@@ -102,6 +102,21 @@
     plus, minus = lax.rem(y + 1, ny), lax.rem(y + ny - 1, ny)
     right, left = index(h, plus, c), index(h, minus, c)
     core, part = index(h, y, 1 - c), index(1 - h, y, c)
+
+    barrier = pltpu.get_barrier_semaphore()
+
+    def signal(**device):
+        pl.semaphore_signal(barrier, inc=1, device_id=device, device_id_type=MESH)
+
+    for k in range(1, nd):
+        signal(die=lax.rem(me + k, nd))
+    for g in (up, down):
+        for d in (west, me, east):
+            signal(grp=g, die=d)
+    for g in (right, left, core):
+        signal(grp=g)
+    for k in range(nd):
+        signal(grp=part, die=lax.rem(me + k, nd))
 
     own = pl.ds(128, blocks)
     own_lanes = slice(128, 128 + blocks)
@@ -117,26 +132,15 @@
                 (volt_hbm, volt_ref),
                 (load_hbm, load_ref),
                 (coup_hbm, coup_ref),
+                (node_hbm, node_ref),
+                (cond_hbm, cond_ref),
+                (block_hbm, block_ref),
             )
         )
     ]
-    for copy in loads:
-        copy.start()
-
-    barrier = pltpu.get_barrier_semaphore()
-
-    def signal(**device):
-        pl.semaphore_signal(barrier, inc=1, device_id=device, device_id_type=MESH)
-
-    for k in range(1, nd):
-        signal(die=lax.rem(me + k, nd))
-    for g in (up, down):
-        for d in (west, me, east):
-            signal(grp=g, die=d)
-    for g in (right, left, core):
-        signal(grp=g)
-    for k in range(nd):
-        signal(grp=part, die=lax.rem(me + k, nd))
+    for copy in loads[::-1]:
+        copy.start()
+    loads[10].wait()
 
     for s in range(nblk):
         ids_out[s // cap, s % cap : s % cap + 1, :] = jnp.full((1, 128), block_ref[s], jnp.int32)
@@ -153,6 +157,7 @@
             onecol[it * chunk + i] = jnp.where(iota == col[i : i + 1, :], 1.0, 0.0).astype(BF16)
         return carry
 
+    loads[8].wait()
     lax.fori_loop(0, steps, one_columns, 0)
     pl.semaphore_wait(barrier, (nd - 1) + 6 + 3 + nd)
 
@@ -216,6 +221,7 @@
         lax.fori_loop(0, steps // 2, double, 0)
 
     loads[4].wait()
+    loads[9].wait()
     scatter(lambda at: jnp.where(node_ref[at, :] >= 0, cond_ref[at, :], 0.0), 0)
 
     def halo_copies(en, es, ew, ee, n, s, w, e, nw, ne, sw, se, sems):
@@ -363,8 +369,6 @@
         v = jnp.where(inside, v + weight * ((r + beside) * inv - v), 0.0)
     final = v[middle]
     die_v[...] = final
-    die_done = pltpu.make_async_copy(die_v, die_hbm, sem_outs.at[0])
-    die_done.start()
     halves = jnp.concatenate(split(final), axis=0)
 
     def currents(it, carry):
@@ -458,20 +462,11 @@
             if nblk < 64:
                 flows.append(jnp.zeros((64 - nblk, 128), F32))
         rhs = jnp.concatenate(split(jnp.concatenate(flows, axis=0)), axis=1)
-        planes[0:256, :] = rhs
-
-        depth = min(blocks, 512)
-
-        def step(q, carry):
-            at = pl.ds(pl.multiple_of(q * depth, depth), depth)
-            target = lax.broadcasted_iota(jnp.int32, (depth, 128), 0) + q * depth
-            lhs = jnp.concatenate(
-                [jnp.where(target == i, 1.0, 0.0).astype(BF16) for i in pair_ids], axis=1
-            )
-            total[at, :] += jnp.dot(lhs, planes[0:256, :], preferred_element_type=F32)
-            return carry
-
-        lax.fori_loop(0, blocks // depth, step, 0)
+        target = lax.broadcasted_iota(jnp.int32, (blocks, 128), 0)
+        lhs = jnp.concatenate(
+            [jnp.where(target == i, 1.0, 0.0).astype(BF16) for i in pair_ids], axis=1
+        )
+        total[...] += jnp.dot(lhs, rhs, preferred_element_type=F32)
 
     def keys_of(dist):
         keys = [
@@ -558,7 +553,7 @@
         coupled = coupled[:, :128] + coupled[:, 128:]
         value = (-inf_x[at, :] - coupled) * rdiag[at, :]
         if iteration == ITERS:
-            x_f[at, :] = value
+            plane_v[start - 128 : start, :] = value
         x_s[iteration, pl.ds(start + 64, 128), :] = jnp.concatenate(split(value), axis=1)
 
     def pairs(iteration, begin, end):
@@ -574,8 +569,6 @@
     for iteration in range(1, ITERS + 1):
         pairs(iteration, 1 if iteration == ITERS else 0, min(iteration, deep))
 
-    plane_done = pltpu.make_async_copy(x_f.at[own], plane_hbm, sem_outs.at[1])
-    plane_done.start()
     rows_x.drain()
     pick_rows(x_s.at[ITERS], 64 + 128, start_ref)
     for j in range(nd):
@@ -590,12 +583,7 @@
     bump_x.wait()
     for j in range(nd):
         bump_v[j * cap : (j + 1) * cap, :] = rows_got[j]
-    bump_done = pltpu.make_async_copy(bump_v, bump_hbm, sem_outs.at[2])
-    bump_done.start()
     bump_x.drain()
-    die_done.wait()
-    plane_done.wait()
-    bump_done.wait()
 
 
 def local(
@@ -609,7 +597,6 @@
     rows, cols = die_volt.shape
     ext = blocks + 256
     knb = pkg_pattern.shape[0]
-    vmem = pl.BlockSpec(memory_space=pltpu.VMEM)
     anywhere = pl.BlockSpec(memory_space=pl.ANY)
     dma = pltpu.SemaphoreType.DMA
 
@@ -626,15 +613,15 @@
     results = pl.pallas_call(
         functools.partial(kernel, nd, ng, cap, blocks),
         out_shape=(
-            jax.ShapeDtypeStruct((rows, cols), F32),
-            jax.ShapeDtypeStruct((blocks, 128), F32),
-            jax.ShapeDtypeStruct((nblk, 128), F32),
+            pltpu.VMEM((rows, cols), F32),
+            pltpu.VMEM((blocks, 128), F32),
+            pltpu.VMEM((nblk, 128), F32),
         ),
-        in_specs=[pl.BlockSpec(memory_space=pltpu.SMEM), vmem, vmem] + [anywhere] * 8,
-        out_specs=(anywhere,) * 3,
+        in_specs=[anywhere] * 11,
+        out_specs=(pl.BlockSpec(memory_space=pltpu.VMEM),) * 3,
         scratch_shapes=[
+            pltpu.SMEM((nblk,), jnp.int32), buf(nblk, 128, dtype=jnp.int32), buf(nblk, 128),
             buf(rows, cols), buf(rows, cols), buf(rows, cols), buf(128, 128),
-            buf(rows, cols), buf(nblk, 128),
             buf(nd, cap, 128, dtype=jnp.int32), buf(nd, cap, 128, dtype=jnp.int32),
             buf(nd, cap, 128), buf(nd, cap, 128),
             buf(nd, cap, 128), buf(nd, cap, 128), buf(nd, cap, 128),
@@ -647,14 +634,13 @@
             *strip_set(16),
             *strip_set(8),
             buf(ng, nblk + 8, 128),
-            buf(ext, 128),
             buf(ITERS + 1, ext + 128, 256, dtype=BF16),
             buf(ext, 128),
             buf(ext, 128), buf(ext, 128), buf(ext, 128),
             buf(knb, ext, dtype=jnp.int32), buf(knb, ext),
             buf(ext // 128, 256, 256, dtype=BF16),
             buf(blocks, 256),
-            dma((8,)), dma((3,)), dma((2, nd)), dma((2, nd)), dma((2, nd)), dma((2, nd)),
+            dma((11,)), dma((2, nd)), dma((2, nd)), dma((2, nd)), dma((2, nd)),
             dma((2, 8)), dma((2, 8)), dma((2, 8)), dma((2,)),
             dma((2, 2, ng // 8 + 2, 2)), dma((2, ng // 2)), dma((2, 2)), dma((2, nd)),
         ],
@@ -667,34 +653,25 @@
     return pl.pallas_call(
         hand_over,
         out_shape=tuple(jax.ShapeDtypeStruct(r.shape, F32) for r in results),
-        in_specs=[anywhere] * 3,
+        in_specs=[pl.BlockSpec(memory_space=pltpu.VMEM)] * 3,
         out_specs=(anywhere,) * 3,
-        scratch_shapes=[buf(*r.shape) for r in results] + [dma((2, 16))],
+        scratch_shapes=[dma((16,))],
         name="hand_over",
-    )(*results)
+    )(*[pltpu.with_memory_space_constraint(r, pltpu.VMEM) for r in results])
 
 
 def hand_over(*refs):
-    sources, targets, held, sem = refs[:3], refs[3:6], refs[6:9], refs[9]
-    pieces = []
-    for k, (src, dst, mid) in enumerate(zip(sources, targets, held)):
+    sources, targets, sem = refs[:3], refs[3:6], refs[6]
+    copies = []
+    for k, (src, dst) in enumerate(zip(sources, targets)):
         count = 8 if k == 1 else 2
         depth = src.shape[0] // count
         for p in range(count):
             at = pl.ds(p * depth, depth)
-            pieces.append((src.at[at], mid.at[at], dst.at[at]))
-    takes = [
-        pltpu.make_async_copy(src, mid, sem.at[0, n]) for n, (src, mid, _) in enumerate(pieces)
-    ]
-    gives = [
-        pltpu.make_async_copy(mid, dst, sem.at[1, n]) for n, (_, mid, dst) in enumerate(pieces)
-    ]
-    for copy in takes:
-        copy.start()
-    for take, give in zip(takes, gives):
-        take.wait()
-        give.start()
-    for copy in gives:
+            copies.append(pltpu.make_async_copy(src.at[at], dst.at[at], sem.at[len(copies)]))
+    for copy in copies:
+        copy.start()
+    for copy in copies:
         copy.wait()
 
 

time: 72.6 us -> 70 us (0.964)
  Pallas kernels: 71.5 us -> 69.1 us
    pallas_call x1, Pallas kernels: 69.5 us -> 68.1 us  [local(): pl.pallas_call(functools.partial(kernel, nd, ng, cap, blocks), out_shape=...]
    pallas_call x1, Pallas kernels: 2.03 us -> 0.97 us  [local(): pl.pallas_call(hand_over, out_shape=tuple((jax.ShapeDtypeStruct(r.shape,...]
where the time goes in v4:
time: 70 us; the launch traced here: 69.8 us
  Pallas kernels  69.1 us (99%)
    pallas_call x1, Pallas kernels, local(): pl.pallas_call(functools.partial(kernel, nd, ng, cap, blocks), out_shape=...  68.1 us

profile of v4, /device:TPU:1, one launch (start us, length us, event | category | flops | bytes accessed | tf_op | source)
XLA Modules:
  0.0 69.8 jit_solution(8580431794746912279)
XLA Ops:
  0.6 68.1 %coupling_round.1 = (f32[128,256]{1,0:T(8,128)S(1)}, f32[1024,128]{1,0:T(8,128)S(1)}, f32[64,128]{1,0:T(8,128)S(1)}) custom-call(s32[64]{0:T(128)} %block_hbm.1, s32[64,128]{1,0:T(8,128)} %node_hbm.1, f32[64,128]{1,0:T(8,128)} %cond_hbm.1, f32[128,256]{1,0:T(8,128)} %volt_hbm.1, f32[128,256]{1,0:T(8,128)} %load_hbm.1, f32[128,256]{1,0:T(8,128)} %shunt_hbm.1, ...), custom_call_target="tpu_custom_call" | custom-call | tf_op jit(solution)/shard_map/coupling_round/pallas_call | solution.py:613
  68.8 1.0 %hand_over.1 = (f32[128,256]{1,0:T(8,128)}, f32[1024,128]{1,0:T(8,128)}, f32[64,128]{1,0:T(8,128)}) custom-call(f32[128,256]{1,0:T(8,128)S(1)} %get-tuple-element.6.refs_0_, f32[1024,128]{1,0:T(8,128)S(1)} %get-tuple-element.7.refs_1_, f32[64,128]{1,0:T(8,128)S(1)} %get-tuple-element.8.refs_2_), custom_call_target="tpu_custom_call" | custom-call | tf_op jit(solution)/shard_map/hand_over/pallas_call | solution.py:653

commit v5 on v4

--- a/solution.py
+++ b/solution.py
@@ -113,7 +113,11 @@
     for g in (up, down):
         for d in (west, me, east):
             signal(grp=g, die=d)
-    for g in (right, left, core):
+    for g in (
+        right, left, core,
+        index(h, lax.rem(y + 2, ny), c),
+        index(h, lax.rem(y + ny - 2, ny), c),
+    ):
         signal(grp=g)
     for k in range(nd):
         signal(grp=part, die=lax.rem(me + k, nd))
@@ -159,7 +163,7 @@
 
     loads[8].wait()
     lax.fori_loop(0, steps, one_columns, 0)
-    pl.semaphore_wait(barrier, (nd - 1) + 6 + 3 + nd)
+    pl.semaphore_wait(barrier, (nd - 1) + 6 + 5 + nd)
 
     ids = Exchange(nd, me, ids_out, ids_got, sem_ids)
     ids.start()
@@ -421,11 +425,14 @@
     sent = []
     core_of = {}
 
-    def pass_on(slot, direction, dist, k):
+    def ahead(direction, hops, cc):
+        return index(h, lax.rem(y + (hops if direction == 0 else ny - hops), ny), cc)
+
+    def pass_on(slot, direction, dist, k, hops=1):
         copy = remote(
             items.at[slot], items.at[slot],
             sem_ring.at[0, direction, dist, k], sem_ring.at[1, direction, dist, k],
-            grp=right if direction == 0 else left,
+            grp=ahead(direction, hops, c),
         )
         copy.start()
         sent.append(copy)
@@ -497,6 +504,9 @@
     for j in range(nd):
         items[mg, j * cap : (j + 1) * cap, :] = cur_got[j]
     for direction in range(2):
+        if reach[direction, 0] >= 2:
+            pass_on(mg, direction, 2, 0, 2)
+    for direction in range(2):
         if reach[direction, 0] >= 1:
             pass_on(mg, direction, 1, 0)
     to_core(mg, "own")
@@ -505,10 +515,14 @@
     for j in range(nd):
         items[part, j * cap : (j + 1) * cap, :] = cur_part[j]
     for direction in range(2):
+        if reach[direction, 1] >= 2:
+            pass_on(part, direction, 2, 1, 2)
+    for direction in range(2):
         if reach[direction, 1] >= 1:
             pass_on(part, direction, 1, 1)
     to_core(part, "part")
-    for dist in range(1, half + 1):
+    order = [2, 1, *range(3, half + 1)] if half > 1 else [1]
+    for step, dist in enumerate(order):
         for k in range(2):
             for direction in range(2):
                 if reach[direction, k] >= dist:
@@ -518,13 +532,15 @@
                         sem_ring.at[0, direction, dist, k], sem_ring.at[1, direction, dist, k],
                         grp=right if direction == 0 else left,
                     ).wait_recv()
-                    if reach[direction, k] >= dist + 1:
-                        pass_on(slot, direction, dist + 1, k)
+                    if dist == 2:
+                        for hops in (2, 1):
+                            if reach[direction, k] >= dist + hops:
+                                pass_on(slot, direction, dist + hops, k, hops)
                     to_core(slot, (direction, dist, k))
         add_group(group(dist, c))
-        if dist > 1:
-            core_group(dist - 1)
-    core_group(half)
+        if step > 0:
+            core_group(order[step - 1])
+    core_group(order[-1])
 
     inf_x[own, :] = total[:, :128] + total[:, 128:]
     infs = [

time: 70 us -> 67 us (0.957)
  Pallas kernels: 69.1 us -> 66.2 us
    pallas_call x1, Pallas kernels: 68.1 us -> 65.2 us  [local(): pl.pallas_call(functools.partial(kernel, nd, ng, cap, blocks), out_shape=...]
where the time goes in v5:
time: 67 us; the launch traced here: 66.9 us
  Pallas kernels  66.2 us (99%)
    pallas_call x1, Pallas kernels, local(): pl.pallas_call(functools.partial(kernel, nd, ng, cap, blocks), out_shape=...  65.2 us

profile of v5, /device:TPU:1, one launch (start us, length us, event | category | flops | bytes accessed | tf_op | source)
XLA Modules:
  0.0 66.9 jit_solution(8647570197105028041)
XLA Ops:
  0.6 65.2 %coupling_round.1 = (f32[128,256]{1,0:T(8,128)S(1)}, f32[1024,128]{1,0:T(8,128)S(1)}, f32[64,128]{1,0:T(8,128)S(1)}) custom-call(s32[64]{0:T(128)} %block_hbm.1, s32[64,128]{1,0:T(8,128)} %node_hbm.1, f32[64,128]{1,0:T(8,128)} %cond_hbm.1, f32[128,256]{1,0:T(8,128)} %volt_hbm.1, f32[128,256]{1,0:T(8,128)} %load_hbm.1, f32[128,256]{1,0:T(8,128)} %shunt_hbm.1, ...), custom_call_target="tpu_custom_call" | custom-call | tf_op jit(solution)/shard_map/coupling_round/pallas_call | solution.py:629
  65.9 1.0 %hand_over.1 = (f32[128,256]{1,0:T(8,128)}, f32[1024,128]{1,0:T(8,128)}, f32[64,128]{1,0:T(8,128)}) custom-call(f32[128,256]{1,0:T(8,128)S(1)} %get-tuple-element.6.refs_0_, f32[1024,128]{1,0:T(8,128)S(1)} %get-tuple-element.7.refs_1_, f32[64,128]{1,0:T(8,128)S(1)} %get-tuple-element.8.refs_2_), custom_call_target="tpu_custom_call" | custom-call | tf_op jit(solution)/shard_map/hand_over/pallas_call | solution.py:669
